TPU v7x, 256 devices: a whole 4x4x8 slice. The times are simulated.
256 devices in a mesh: sky: 64 (over z, y, core), rep: 4 (over x).
Axes of the slice: x: 4, y: 4, z: 8, core: 2. Of those that a mesh axis runs over, the one named last changes fastest.
Arguments:
- saved_acts: bfloat16 [64, 1024, 2048], P('rep', 'sky'), parts along dimension 0, may hold values from -4 to 4
- scales: float32 [64, 1024, 16], P('rep', 'sky'), parts along dimension 0, may hold values from 0.2 to 4
- grad_out: bfloat16 [64, 1024, 2048], P('rep', 'sky'), parts along dimension 0, may hold values from -6 to 6
- weights: bfloat16 [5, 16, 16], replicated, may hold values from -0.625 to 0.625
- edge_up: int32 [64, 3, 2048], P('sky'), may hold values from 0 to 2048, as said below
- edge_down: int32 [64, 3, 2048], P('sky'), may hold values from 0 to 2048, as said below
Outputs:
- grad_in: bfloat16 [64, 1024, 2048], P('rep', 'sky'), parts along dimension 0
- weight_grad: float32 [20, 16, 16], P('rep'), parts along dimension 0
There are 4 independent parts, one for each index of `rep`. A program takes and returns all parts, laid end to end along the dimension named above; an argument that names none is the same for every part. Nothing has to cross between parts.
Inputs may be any that keep to these rules, and one draw needn't show every extreme that they name: edge_down[t, j, c] is the column of tile t+1's first row (tile 0 after the last) linked to column c of tile t's last row, or 2048 where there is none; the links are mutual: edge_up of tile t+1 lists exactly the reverse links. edge_up[t, j, c] is the column of tile t-1's last row (the last tile before tile 0) linked to column c of tile t's first row, or 2048 where there is none.
All inputs are finite; a program needn't handle non-finite values.
Results may differ from a plain program's by a relative error of at most 0.0028.
Values sent between devices are 32-bit elements; how exact they have to be, the bound alone decides.
A program may use at most 192 MiB of HBM per device.

v0:
```python
import math

import jax
import jax.numpy as jnp
from jax import lax
from jax.sharding import PartitionSpec as P


def extended_2(block, sides, width):
    for axis, dim in sides:
        count = lax.axis_size(axis)
        forward = [(i, i + 1) for i in range(count - 1)]
        forward.append((count - 1, 0))
        backward = [(target, source) for source, target in forward]
        low = lax.ppermute(
            lax.slice_in_dim(block, block.shape[dim] - width, None, axis=dim), axis, forward
        )
        high = lax.ppermute(lax.slice_in_dim(block, 0, width, axis=dim), axis, backward)
        block = jnp.concatenate([low, block, high], axis=dim)
    return block


def triple(field_rows):
    padded = jnp.pad(field_rows, ((0, 0), (0, 0), (1, 1)))
    return padded[:, :, :-2] + padded[:, :, 1:-1] + padded[:, :, 2:]


def link_matrix(link_lists, row_width):
    sources = jnp.arange(row_width, dtype=jnp.int32)[:, None]
    matrix = jnp.zeros((row_width, row_width), jnp.bfloat16)
    for column in range(3):
        matrix = matrix + (sources == link_lists[column][None, :]).astype(jnp.bfloat16)
    return matrix


def linked_row(edge_row, matrix):
    channels = edge_row.shape[0]
    high = edge_row.astype(jnp.bfloat16)
    rest = edge_row - high.astype(jnp.float32)
    middle_part = rest.astype(jnp.bfloat16)
    low = (rest - middle_part.astype(jnp.float32)).astype(jnp.bfloat16)
    stacked = jnp.concatenate([high, middle_part, low], axis=0)
    product = jnp.dot(stacked, matrix, preferred_element_type=jnp.float32)
    return product[:channels] + product[channels : 2 * channels] + product[2 * channels :]


def stencil(extended, above_links, below_links):
    row_above = extended[:, :-2]
    middle = extended[:, 1:-1]
    row_below = extended[:, 2:]
    vert_above = triple(row_above)
    for where_row, matrix in above_links:
        vert_above = vert_above.at[:, where_row].set(linked_row(row_above[:, where_row], matrix))
    vert_below = triple(row_below)
    for where_row, matrix in below_links:
        vert_below = vert_below.at[:, where_row].set(linked_row(row_below[:, where_row], matrix))
    return -0.125 * (vert_above + vert_below + (triple(middle) - middle))


def on_device(saved_acts, scales, grad_out, weights, edge_up, edge_down):
    channels, tile_rows, columns = saved_acts.shape
    orders = weights.shape[0]
    blocks = scales.shape[2]
    up_matrix = link_matrix(edge_up[0], columns)
    down_matrix = link_matrix(edge_down[0], columns)
    activation = (
        saved_acts.astype(jnp.float32).reshape(channels, tile_rows, blocks, columns // blocks)
        * scales[..., None]
    ).reshape(channels, tile_rows, columns)

    def extend_each(state):
        return extended_2(state, (("sky", 1),), 1)

    coeff_terms = jnp.einsum("kio,orc->kirc", weights, grad_out, preferred_element_type=jnp.float32)
    cheb_terms = [activation]
    current = coeff_terms[orders - 1]
    previous = jnp.zeros_like(current)
    for sweep in range(orders - 1):
        both = jnp.concatenate([extend_each(cheb_terms[-1]), extend_each(current)], axis=0)
        images = stencil(both, ((0, up_matrix),), ((tile_rows - 1, down_matrix),))
        forward_image = images[:channels]
        backward_image = images[channels:]
        if sweep == 0:
            cheb_terms.append(forward_image)
        else:
            cheb_terms.append(2.0 * forward_image - cheb_terms[-2])
        position = orders - 2 - sweep
        if position >= 1:
            updated = coeff_terms[position] + 2.0 * backward_image - previous
        else:
            updated = coeff_terms[0] + backward_image - previous
        previous, current = (current, updated)
    grad_in = current.astype(jnp.bfloat16)
    rounded = jnp.stack([term.astype(jnp.bfloat16) for term in cheb_terms])
    local_sums = jnp.einsum("kirc,orc->kio", rounded, grad_out, preferred_element_type=jnp.float32)
    summed = lax.psum(local_sums, "sky")
    weight_grad = summed * (1.0 / math.sqrt(tile_rows * columns * lax.axis_size("sky")))
    return (grad_in, weight_grad)


def solution(mesh):
    return jax.shard_map(
        on_device,
        mesh=mesh,
        in_specs=(
            P("rep", "sky", None),
            P("rep", "sky", None),
            P("rep", "sky", None),
            P(),
            P("sky", None, None),
            P("sky", None, None),
        ),
        out_specs=(P("rep", "sky", None), P("rep", None, None)),
        check_vma=False,
    )
```

profile of v0, /device:TPU:4, one launch (start us, length us, event | category | flops | bytes accessed | tf_op | source)
XLA Modules:
  0.0 475.0 jit_solution(9159034872456606348)
XLA Ops:
  1.4 2.8 fusion.76
  4.2 4.0 copy-done.2
  10.5 7.7 %collective-permute-start.3 = (f32[16,1,2048]{2,0,1:T(8,128)}, f32[16,1,2048]{2,0,1:T(8,128)S(1)}, u32[]{:S(2)}, u32[]{:S(2)}) collective-permute-start(f32[16,1,2048]{2,0,1:T(8,128)} %get-tuple-element.159), channel_id=1, source_target_pairs={{4,0},{8,4},{12,8},{16,12},{20,16},{24,20},{28,24},{32,28},{36,32}... | collective-permute-start | bytes 393224 | tf_op jit(solution)/shard_map/ppermute | solution.py:18
  18.3 2.1 mul.47
  20.3 1.7 mul.48
  22.1 1.7 bitcast_dynamic-update-slice_fusion.3
  23.9 5.1 %collective-permute-start.1 = (f32[16,1,2048]{2,0,1:T(8,128)S(1)}, f32[16,1,2048]{2,0,1:T(8,128)S(1)}, u32[]{:S(2)}, u32[]{:S(2)}) collective-permute-start(f32[16,1,2048]{2,0,1:T(8,128)S(1)} %get-tuple-element.157), channel_id=1, source_target_pairs={{4,0},{8,4},{12,8},{16,12},{20,16},{24,20},{28,24},{32,28},{36,32}... | collective-permute-start | bytes 393224 | tf_op jit(solution)/shard_map/ppermute | solution.py:18
  29.0 2.5 collective-permute-done.1
  31.5 5.2 %collective-permute-done = f32[16,1,2048]{2,0,1:T(8,128)S(1)} collective-permute-done((f32[16,1,2048]{2,0,1:T(8,128)S(1)}, f32[16,1,2048]{2,0,1:T(8,128)S(1)}, u32[]{:S(2)}, u32[]{:S(2)}) %collective-permute-start) | collective-permute-done | bytes 131104 | tf_op jit(solution)/shard_map/ppermute | solution.py:15
  37.1 4.8 %fusion.166 = (f32[32,16,2048]{2,0,1:T(8,128)}, f32[32,16,2048]{2,0,1:T(8,128)}, f32[32,16,2048]{2,0,1:T(8,128)}) fusion(f32[32,18,2048]{2,0,1:T(8,128)S(1)} %maximum_maximum_fusion), kind=kLoop, calls=%fused_computation.249 | loop fusion | bytes 25165824 | tf_op jit(solution)/shard_map/slice | solution.py:50
  41.9 14.0 %fusion.27 = (f32[32,16,2048]{2,0,1:T(8,128)S(1)}, f32[32,16,2048]{2,0,1:T(8,128)S(1)}) fusion(f32[32,16,2048]{2,0,1:T(8,128)} %get-tuple-element.141, f32[32,16,2048]{2,0,1:T(8,128)} %get-tuple-element.139), kind=kLoop, calls=%fused_computation.53 | loop fusion | flops 4194304 | bytes 16777216 | tf_op jit(solution)/shard_map/add | solution.py:25
  56.1 6.4 %fusion.24 = f32[96,2048]{1,0:T(8,128)S(1)} fusion(s32[2048]{0:T(1024)S(1)} %bitcast.131, s32[2048]{0:T(1024)S(1)} %bitcast.135, s32[2048]{0:T(1024)S(1)} %bitcast.127, bf16[32,2048]{1,0:T(8,128)(2,1)S(1)} %get-tuple-element.175, bf16[32,2048]{1,0:T(8,128)(2,1)S(1)} %get-tuple-element.174, bf16[32,2048]{1,0:T(8,128)(2,1)S(1)} %get-tuple-element.137), kind=kOutput, calls=%fused_computation.23 | convolution fusion | flops 856817664 | bytes 1204224 | tf_op jit(solution)/shard_map/dot_general | solution.py:43
  62.5 6.6 %fusion.16 = f32[96,2048]{1,0:T(8,128)S(1)} fusion(s32[2048]{0:T(1024)S(1)} %bitcast.119, s32[2048]{0:T(1024)S(1)} %bitcast.123, s32[2048]{0:T(1024)S(1)} %bitcast.115, bf16[32,2048]{1,0:T(8,128)(2,1)S(1)} %get-tuple-element.184, bf16[32,2048]{1,0:T(8,128)(2,1)S(1)} %get-tuple-element.185, bf16[32,2048]{1,0:T(8,128)(2,1)S(1)} %get-tuple-element.118), kind=kOutput, calls=%fused_computation.19 | convolution fusion | flops 856817664 | bytes 1204224 | tf_op jit(solution)/shard_map/dot_general | solution.py:43
  69.2 2.8 fusion.34
  72.0 3.6 fusion.168
  76.2 4.6 collective-permute-start.5
  83.5 5.1 %collective-permute-done.4 = f32[16,1,2048]{2,0,1:T(8,128)S(1)} collective-permute-done((f32[16,1,2048]{2,0,1:T(8,128)S(1)}, f32[16,1,2048]{2,0,1:T(8,128)S(1)}, u32[]{:S(2)}, u32[]{:S(2)}) %collective-permute-start.4) | collective-permute-done | bytes 131104 | tf_op jit(solution)/shard_map/ppermute | solution.py:15
  89.2 4.8 %fusion.165 = (f32[32,16,2048]{2,0,1:T(8,128)}, f32[32,16,2048]{2,0,1:T(8,128)}, f32[32,16,2048]{2,0,1:T(8,128)}) fusion(f32[32,18,2048]{2,0,1:T(8,128)S(1)} %maximum_maximum_fusion.1), kind=kLoop, calls=%fused_computation.248 | loop fusion | bytes 25165824 | tf_op jit(solution)/shard_map/slice | solution.py:50
  94.0 7.0 %fusion.36 = f32[32,16,2048]{2,0,1:T(8,128)S(1)} fusion(f32[32,16,2048]{2,0,1:T(8,128)} %get-tuple-element.136), kind=kLoop, calls=%fused_computation.62 | loop fusion | flops 2097152 | bytes 8388608 | tf_op jit(solution)/shard_map/add | solution.py:25
  101.1 2.1 copy-done.27
  103.2 2.2 fusion.38
  105.5 6.4 %fusion.22 = f32[96,2048]{1,0:T(8,128)S(1)} fusion(s32[2048]{0:T(1024)S(1)} %bitcast.132, s32[2048]{0:T(1024)S(1)} %bitcast.136, s32[2048]{0:T(1024)S(1)} %bitcast.128, bf16[32,2048]{1,0:T(8,128)(2,1)S(1)} %get-tuple-element.171, bf16[32,2048]{1,0:T(8,128)(2,1)S(1)} %get-tuple-element.170, bf16[32,2048]{1,0:T(8,128)(2,1)S(1)} %get-tuple-element.132), kind=kOutput, calls=%fused_computation.22 | convolution fusion | flops 856817664 | bytes 1204224 | tf_op jit(solution)/shard_map/dot_general | solution.py:43
  111.9 6.8 %fusion.14 = f32[96,2048]{1,0:T(8,128)S(1)} fusion(s32[2048]{0:T(1024)S(1)} %bitcast.120, s32[2048]{0:T(1024)S(1)} %bitcast.124, s32[2048]{0:T(1024)S(1)} %bitcast.116, bf16[32,2048]{1,0:T(8,128)(2,1)S(1)} %get-tuple-element.169, bf16[32,2048]{1,0:T(8,128)(2,1)S(1)} %get-tuple-element.168, bf16[32,2048]{1,0:T(8,128)(2,1)S(1)} %get-tuple-element.114), kind=kOutput, calls=%fused_computation.18 | convolution fusion | flops 856817664 | bytes 1204224 | tf_op jit(solution)/shard_map/dot_general | solution.py:43
  118.8 2.8 fusion.43
  121.6 2.8 fusion.70
  126.5 4.7 collective-permute-start.9
  133.7 5.2 %collective-permute-done.8 = f32[16,1,2048]{2,0,1:T(8,128)S(1)} collective-permute-done((f32[16,1,2048]{2,0,1:T(8,128)S(1)}, f32[16,1,2048]{2,0,1:T(8,128)S(1)}, u32[]{:S(2)}, u32[]{:S(2)}) %collective-permute-start.8) | collective-permute-done | bytes 131104 | tf_op jit(solution)/shard_map/ppermute | solution.py:15
  139.5 4.8 %fusion.164 = (f32[32,16,2048]{2,0,1:T(8,128)}, f32[32,16,2048]{2,0,1:T(8,128)}, f32[32,16,2048]{2,0,1:T(8,128)}) fusion(f32[32,18,2048]{2,0,1:T(8,128)S(1)} %maximum_maximum_fusion.2), kind=kLoop, calls=%fused_computation.247 | loop fusion | bytes 25165824 | tf_op jit(solution)/shard_map/slice | solution.py:50
  144.2 7.0 %fusion.45 = f32[32,16,2048]{2,0,1:T(8,128)S(1)} fusion(f32[32,16,2048]{2,0,1:T(8,128)} %get-tuple-element.131), kind=kLoop, calls=%fused_computation.71 | loop fusion | flops 2097152 | bytes 8388608 | tf_op jit(solution)/shard_map/add | solution.py:25
  151.4 2.1 copy-done.28
  153.5 2.2 fusion.47
  155.8 6.4 %fusion.20 = f32[96,2048]{1,0:T(8,128)S(1)} fusion(s32[2048]{0:T(1024)S(1)} %bitcast.133, s32[2048]{0:T(1024)S(1)} %bitcast.137, s32[2048]{0:T(1024)S(1)} %bitcast.129, bf16[32,2048]{1,0:T(8,128)(2,1)S(1)} %get-tuple-element.167, bf16[32,2048]{1,0:T(8,128)(2,1)S(1)} %get-tuple-element.166, bf16[32,2048]{1,0:T(8,128)(2,1)S(1)} %get-tuple-element.127), kind=kOutput, calls=%fused_computation.21 | convolution fusion | flops 856817664 | bytes 1204224 | tf_op jit(solution)/shard_map/dot_general | solution.py:43
  162.2 6.6 %fusion.12 = f32[96,2048]{1,0:T(8,128)S(1)} fusion(s32[2048]{0:T(1024)S(1)} %bitcast.121, s32[2048]{0:T(1024)S(1)} %bitcast.125, s32[2048]{0:T(1024)S(1)} %bitcast.117, bf16[32,2048]{1,0:T(8,128)(2,1)S(1)} %get-tuple-element.165, bf16[32,2048]{1,0:T(8,128)(2,1)S(1)} %get-tuple-element.164, bf16[32,2048]{1,0:T(8,128)(2,1)S(1)} %get-tuple-element.110), kind=kOutput, calls=%fused_computation.17 | convolution fusion | flops 856817664 | bytes 1204224 | tf_op jit(solution)/shard_map/dot_general | solution.py:43
  168.9 2.8 fusion.52
  171.7 2.2 fusion.67
  176.0 4.7 collective-permute-start.13
  183.3 5.2 %collective-permute-done.12 = f32[16,1,2048]{2,0,1:T(8,128)S(1)} collective-permute-done((f32[16,1,2048]{2,0,1:T(8,128)S(1)}, f32[16,1,2048]{2,0,1:T(8,128)S(1)}, u32[]{:S(2)}, u32[]{:S(2)}) %collective-permute-start.12) | collective-permute-done | bytes 131104 | tf_op jit(solution)/shard_map/ppermute | solution.py:15
  189.2 4.8 %fusion.163 = (f32[32,16,2048]{2,0,1:T(8,128)}, f32[32,16,2048]{2,0,1:T(8,128)}, f32[32,16,2048]{2,0,1:T(8,128)}) fusion(f32[32,18,2048]{2,0,1:T(8,128)S(1)} %maximum_maximum_fusion.3), kind=kLoop, calls=%fused_computation.246 | loop fusion | bytes 25165824 | tf_op jit(solution)/shard_map/slice | solution.py:50
  194.0 7.0 %fusion.54 = f32[32,16,2048]{2,0,1:T(8,128)S(1)} fusion(f32[32,16,2048]{2,0,1:T(8,128)} %get-tuple-element.126), kind=kLoop, calls=%fused_computation.80 | loop fusion | flops 2097152 | bytes 8388608 | tf_op jit(solution)/shard_map/add | solution.py:25
  201.2 2.1 copy-done.26
  203.2 2.2 fusion.56
  205.5 6.4 %fusion.18 = f32[96,2048]{1,0:T(8,128)S(1)} fusion(s32[2048]{0:T(1024)S(1)} %bitcast.134, s32[2048]{0:T(1024)S(1)} %bitcast.138, s32[2048]{0:T(1024)S(1)} %bitcast.130, bf16[32,2048]{1,0:T(8,128)(2,1)S(1)} %get-tuple-element.163, bf16[32,2048]{1,0:T(8,128)(2,1)S(1)} %get-tuple-element.162, bf16[32,2048]{1,0:T(8,128)(2,1)S(1)} %get-tuple-element.122), kind=kOutput, calls=%fused_computation.20 | convolution fusion | flops 856817664 | bytes 1204224 | tf_op jit(solution)/shard_map/dot_general | solution.py:43
  212.0 6.6 %fusion.10 = f32[96,2048]{1,0:T(8,128)S(1)} fusion(s32[2048]{0:T(1024)S(1)} %bitcast.122, s32[2048]{0:T(1024)S(1)} %bitcast.126, s32[2048]{0:T(1024)S(1)} %bitcast.118, bf16[32,2048]{1,0:T(8,128)(2,1)S(1)} %get-tuple-element.161, bf16[32,2048]{1,0:T(8,128)(2,1)S(1)} %get-tuple-element.160, bf16[32,2048]{1,0:T(8,128)(2,1)S(1)} %get-tuple-element.106), kind=kOutput, calls=%fused_computation.16 | convolution fusion | flops 856817664 | bytes 1204224 | tf_op jit(solution)/shard_map/dot_general | solution.py:43
  218.7 2.8 fusion.61
  221.5 2.3 fusion.65
  223.7 1.5 copy.12
  225.7 2.3 convolution_bitcast_fusion
  228.1 246.1 %psum.7 = f32[5,16,16]{2,1,0:T(8,128)S(1)} all-reduce(f32[5,16,16]{2,1,0:T(8,128)S(1)} %convolution_bitcast_fusion), channel_id=1, replica_groups=mesh['sky'=64,'rep'=4] {'sky'}, use_global_device_ids=true, to_apply=%region_0.1 | all-reduce | flops 1280 | bytes 10240 | tf_op jit(solution)/shard_map/psum | solution.py:96
  (139 shorter events, 19.7 us)
Async XLA Ops:
  4.2 4.0 copy-start.2
  8.2 10.0 %copy-start.35 = (f32[16,16,16]{2,1,0:T(8,128)S(1)}, f32[16,16,16]{2,1,0:T(8,128)}, u32[]{:S(2)}) copy-start(f32[16,16,16]{2,1,0:T(8,128)} %param.23) | copy-start | bytes 49156
  9.8 12.3 %copy-start.34 = (bf16[16,16,2048]{2,1,0:T(8,128)(2,1)S(1)}, bf16[16,16,2048]{2,1,0:T(8,128)(2,1)}, u32[]{:S(2)}) copy-start(bf16[16,16,2048]{2,1,0:T(8,128)(2,1)} %param.22) | copy-start | bytes 3145732
  10.5 18.6 %collective-permute-start.3 = (f32[16,1,2048]{2,0,1:T(8,128)}, f32[16,1,2048]{2,0,1:T(8,128)S(1)}, u32[]{:S(2)}, u32[]{:S(2)}) collective-permute-start(f32[16,1,2048]{2,0,1:T(8,128)} %get-tuple-element.159), channel_id=1, source_target_pairs={{4,0},{8,4},{12,8},{16,12},{20,16},{24,20},{28,24},{32,28},{36,32}... | collective-permute-start | bytes 393224 | tf_op jit(solution)/shard_map/ppermute | solution.py:18
  18.2 10.8 %collective-permute-start.2 = (f32[16,1,2048]{2,0,1:T(8,128)}, f32[16,1,2048]{2,0,1:T(8,128)S(1)}, u32[]{:S(2)}, u32[]{:S(2)}) collective-permute-start(f32[16,1,2048]{2,0,1:T(8,128)} %get-tuple-element.158), channel_id=1, source_target_pairs={{0,4},{4,8},{8,12},{12,16},{16,20},{20,24},{24,28},{28,32},{32,36}... | collective-permute-start | bytes 393224 | tf_op jit(solution)/shard_map/ppermute | solution.py:15
  22.1 6.9 %copy-start.36 = (s32[1,3,2048]{2,0,1:T(1,128)S(1)}, s32[1,3,2048]{2,0,1:T(1,128)}, u32[]{:S(2)}) copy-start(s32[1,3,2048]{2,0,1:T(1,128)} %param.26) | copy-start | bytes 73732
  22.1 6.9 %copy-start.37 = (s32[1,3,2048]{2,0,1:T(1,128)S(1)}, s32[1,3,2048]{2,0,1:T(1,128)}, u32[]{:S(2)}) copy-start(s32[1,3,2048]{2,0,1:T(1,128)} %param.27) | copy-start | bytes 73732
  22.1 14.6 %copy-start.20 = (f32[16,16,2048]{2,0,1:T(8,128)S(1)}, f32[16,16,2048]{2,0,1:T(8,128)}, u32[]{:S(2)}) copy-start(f32[16,16,2048]{2,0,1:T(8,128)} %copy-done.19) | copy-start | bytes 6291460
  23.8 12.9 %copy-start.3 = (f32[16,16,2048]{2,0,1:T(8,128)}, f32[16,16,2048]{2,0,1:T(8,128)S(1)}, u32[]{:S(2)}) copy-start(f32[16,16,2048]{2,0,1:T(8,128)S(1)} %get-tuple-element.105) | copy-start | bytes 6291460
  23.9 7.7 %collective-permute-start.1 = (f32[16,1,2048]{2,0,1:T(8,128)S(1)}, f32[16,1,2048]{2,0,1:T(8,128)S(1)}, u32[]{:S(2)}, u32[]{:S(2)}) collective-permute-start(f32[16,1,2048]{2,0,1:T(8,128)S(1)} %get-tuple-element.157), channel_id=1, source_target_pairs={{4,0},{8,4},{12,8},{16,12},{20,16},{24,20},{28,24},{32,28},{36,32}... | collective-permute-start | bytes 393224 | tf_op jit(solution)/shard_map/ppermute | solution.py:18
  29.0 7.7 %collective-permute-start = (f32[16,1,2048]{2,0,1:T(8,128)S(1)}, f32[16,1,2048]{2,0,1:T(8,128)S(1)}, u32[]{:S(2)}, u32[]{:S(2)}) collective-permute-start(f32[16,1,2048]{2,0,1:T(8,128)S(1)} %get-tuple-element.156), channel_id=1, source_target_pairs={{0,4},{4,8},{8,12},{12,16},{16,20},{20,24},{24,28},{28,32},{32,36}... | collective-permute-start | bytes 393224 | tf_op jit(solution)/shard_map/ppermute | solution.py:15
  41.9 14.0 %copy-start.4 = (f32[16,16,2048]{2,0,1:T(8,128)S(1)}, f32[16,16,2048]{2,0,1:T(8,128)}, u32[]{:S(2)}) copy-start(f32[16,16,2048]{2,0,1:T(8,128)} %copy-done.3) | copy-start | bytes 6291460
  41.9 14.0 %copy-start.21 = (f32[16,16,2048]{2,0,1:T(8,128)S(1)}, f32[16,16,2048]{2,0,1:T(8,128)}, u32[]{:S(2)}) copy-start(f32[16,16,2048]{2,0,1:T(8,128)} %copy-done.19) | copy-start | bytes 6291460
  62.5 6.6 %copy-start.30 = (f32[32,16,2048]{2,0,1:T(8,128)S(1)}, f32[32,16,2048]{2,0,1:T(8,128)}, u32[]{:S(2)}) copy-start(f32[32,16,2048]{2,0,1:T(8,128)} %get-tuple-element.140) | copy-start | bytes 12582916
  72.0 8.9 %copy-start.15 = (f32[32,16,2048]{2,0,1:T(8,128)}, f32[32,16,2048]{2,0,1:T(8,128)S(1)}, u32[]{:S(2)}) copy-start(f32[32,16,2048]{2,0,1:T(8,128)S(1)} %fusion.34) | copy-start | bytes 12582916
  75.6 13.0 %copy-start.12 = (f32[16,16,2048]{2,0,1:T(8,128)}, f32[16,16,2048]{2,0,1:T(8,128)S(1)}, u32[]{:S(2)}) copy-start(f32[16,16,2048]{2,0,1:T(8,128)S(1)} %get-tuple-element.145) | copy-start | bytes 6291460
  75.6 13.0 %copy-start.24 = (f32[16,16,2048]{2,0,1:T(8,128)}, f32[16,16,2048]{2,0,1:T(8,128)S(1)}, u32[]{:S(2)}) copy-start(f32[16,16,2048]{2,0,1:T(8,128)S(1)} %get-tuple-element.144) | copy-start | bytes 6291460
  75.6 6.4 %collective-permute-start.7 = (f32[16,1,2048]{2,0,1:T(8,128)S(1)}, f32[16,1,2048]{2,0,1:T(8,128)S(1)}, u32[]{:S(2)}, u32[]{:S(2)}) collective-permute-start(f32[16,1,2048]{2,0,1:T(8,128)S(1)} %get-tuple-element.155), channel_id=1, source_target_pairs={{4,0},{8,4},{12,8},{16,12},{20,16},{24,20},{28,24},{32,28},{36,32}... | collective-permute-start | bytes 393224 | tf_op jit(solution)/shard_map/ppermute | solution.py:18
  75.7 7.8 %collective-permute-start.6 = (f32[16,1,2048]{2,0,1:T(8,128)S(1)}, f32[16,1,2048]{2,0,1:T(8,128)S(1)}, u32[]{:S(2)}, u32[]{:S(2)}) collective-permute-start(f32[16,1,2048]{2,0,1:T(8,128)S(1)} %get-tuple-element.154), channel_id=1, source_target_pairs={{0,4},{4,8},{8,12},{12,16},{16,20},{20,24},{24,28},{28,32},{32,36}... | collective-permute-start | bytes 393224 | tf_op jit(solution)/shard_map/ppermute | solution.py:15
  76.2 7.3 %collective-permute-start.5 = (f32[16,1,2048]{2,0,1:T(8,128)S(1)}, f32[16,1,2048]{2,0,1:T(8,128)S(1)}, u32[]{:S(2)}, u32[]{:S(2)}) collective-permute-start(f32[16,1,2048]{2,0,1:T(8,128)S(1)} %get-tuple-element.143), channel_id=1, source_target_pairs={{4,0},{8,4},{12,8},{16,12},{20,16},{24,20},{28,24},{32,28},{36,32}... | collective-permute-start | bytes 393224 | tf_op jit(solution)/shard_map/ppermute | solution.py:18
  80.9 7.7 %collective-permute-start.4 = (f32[16,1,2048]{2,0,1:T(8,128)S(1)}, f32[16,1,2048]{2,0,1:T(8,128)S(1)}, u32[]{:S(2)}, u32[]{:S(2)}) collective-permute-start(f32[16,1,2048]{2,0,1:T(8,128)S(1)} %get-tuple-element.142), channel_id=1, source_target_pairs={{0,4},{4,8},{8,12},{12,16},{16,20},{20,24},{24,28},{28,32},{32,36}... | collective-permute-start | bytes 393224 | tf_op jit(solution)/shard_map/ppermute | solution.py:15
  94.0 7.0 %copy-start.13 = (f32[16,16,2048]{2,0,1:T(8,128)S(1)}, f32[16,16,2048]{2,0,1:T(8,128)}, u32[]{:S(2)}) copy-start(f32[16,16,2048]{2,0,1:T(8,128)} %copy-done.12) | copy-start | bytes 6291460
  94.0 7.0 %copy-start.25 = (f32[16,16,2048]{2,0,1:T(8,128)S(1)}, f32[16,16,2048]{2,0,1:T(8,128)}, u32[]{:S(2)}) copy-start(f32[16,16,2048]{2,0,1:T(8,128)} %copy-done.24) | copy-start | bytes 6291460
  111.9 6.9 %copy-start.31 = (f32[32,16,2048]{2,0,1:T(8,128)S(1)}, f32[32,16,2048]{2,0,1:T(8,128)}, u32[]{:S(2)}) copy-start(f32[32,16,2048]{2,0,1:T(8,128)} %get-tuple-element.135) | copy-start | bytes 12582916
  121.6 3.5 copy-start.5
  124.4 14.5 %copy-start.6 = (f32[16,16,2048]{2,0,1:T(8,128)}, f32[16,16,2048]{2,0,1:T(8,128)S(1)}, u32[]{:S(2)}) copy-start(f32[16,16,2048]{2,0,1:T(8,128)S(1)} %fusion.70) | copy-start | bytes 6291460
  124.5 6.8 %collective-permute-start.11 = (f32[16,1,2048]{2,0,1:T(8,128)S(1)}, f32[16,1,2048]{2,0,1:T(8,128)S(1)}, u32[]{:S(2)}, u32[]{:S(2)}) collective-permute-start(f32[16,1,2048]{2,0,1:T(8,128)S(1)} %get-tuple-element.153), channel_id=1, source_target_pairs={{4,0},{8,4},{12,8},{16,12},{20,16},{24,20},{28,24},{32,28},{36,32}... | collective-permute-start | bytes 393224 | tf_op jit(solution)/shard_map/ppermute | solution.py:18
  124.6 7.8 %collective-permute-start.10 = (f32[16,1,2048]{2,0,1:T(8,128)S(1)}, f32[16,1,2048]{2,0,1:T(8,128)S(1)}, u32[]{:S(2)}, u32[]{:S(2)}) collective-permute-start(f32[16,1,2048]{2,0,1:T(8,128)S(1)} %get-tuple-element.152), channel_id=1, source_target_pairs={{0,4},{4,8},{8,12},{12,16},{16,20},{20,24},{24,28},{28,32},{32,36}... | collective-permute-start | bytes 393224 | tf_op jit(solution)/shard_map/ppermute | solution.py:15
  126.5 12.5 %copy-start.9 = (f32[16,16,2048]{2,0,1:T(8,128)}, f32[16,16,2048]{2,0,1:T(8,128)S(1)}, u32[]{:S(2)}) copy-start(f32[16,16,2048]{2,0,1:T(8,128)S(1)} %get-tuple-element.103) | copy-start | bytes 6291460
  126.5 7.2 %collective-permute-start.9 = (f32[16,1,2048]{2,0,1:T(8,128)S(1)}, f32[16,1,2048]{2,0,1:T(8,128)S(1)}, u32[]{:S(2)}, u32[]{:S(2)}) collective-permute-start(f32[16,1,2048]{2,0,1:T(8,128)S(1)} %get-tuple-element.151), channel_id=1, source_target_pairs={{4,0},{8,4},{12,8},{16,12},{20,16},{24,20},{28,24},{32,28},{36,32}... | collective-permute-start | bytes 393224 | tf_op jit(solution)/shard_map/ppermute | solution.py:18
  131.2 7.7 %collective-permute-start.8 = (f32[16,1,2048]{2,0,1:T(8,128)S(1)}, f32[16,1,2048]{2,0,1:T(8,128)S(1)}, u32[]{:S(2)}, u32[]{:S(2)}) collective-permute-start(f32[16,1,2048]{2,0,1:T(8,128)S(1)} %get-tuple-element.150), channel_id=1, source_target_pairs={{0,4},{4,8},{8,12},{12,16},{16,20},{20,24},{24,28},{28,32},{32,36}... | collective-permute-start | bytes 393224 | tf_op jit(solution)/shard_map/ppermute | solution.py:15
  144.2 7.0 %copy-start.7 = (f32[16,16,2048]{2,0,1:T(8,128)S(1)}, f32[16,16,2048]{2,0,1:T(8,128)}, u32[]{:S(2)}) copy-start(f32[16,16,2048]{2,0,1:T(8,128)} %copy-done.6) | copy-start | bytes 6291460
  144.2 7.0 %copy-start.10 = (f32[16,16,2048]{2,0,1:T(8,128)S(1)}, f32[16,16,2048]{2,0,1:T(8,128)}, u32[]{:S(2)}) copy-start(f32[16,16,2048]{2,0,1:T(8,128)} %copy-done.9) | copy-start | bytes 6291460
  162.2 6.7 %copy-start.32 = (f32[32,16,2048]{2,0,1:T(8,128)S(1)}, f32[32,16,2048]{2,0,1:T(8,128)}, u32[]{:S(2)}) copy-start(f32[32,16,2048]{2,0,1:T(8,128)} %get-tuple-element.130) | copy-start | bytes 12582916
  171.7 2.9 copy-start.16
  174.0 14.5 %copy-start.22 = (f32[16,16,2048]{2,0,1:T(8,128)}, f32[16,16,2048]{2,0,1:T(8,128)S(1)}, u32[]{:S(2)}) copy-start(f32[16,16,2048]{2,0,1:T(8,128)S(1)} %fusion.67) | copy-start | bytes 6291460
  174.0 6.8 %collective-permute-start.15 = (f32[16,1,2048]{2,0,1:T(8,128)S(1)}, f32[16,1,2048]{2,0,1:T(8,128)S(1)}, u32[]{:S(2)}, u32[]{:S(2)}) collective-permute-start(f32[16,1,2048]{2,0,1:T(8,128)S(1)} %get-tuple-element.149), channel_id=1, source_target_pairs={{4,0},{8,4},{12,8},{16,12},{20,16},{24,20},{28,24},{32,28},{36,32}... | collective-permute-start | bytes 393224 | tf_op jit(solution)/shard_map/ppermute | solution.py:18
  174.1 7.8 %collective-permute-start.14 = (f32[16,1,2048]{2,0,1:T(8,128)S(1)}, f32[16,1,2048]{2,0,1:T(8,128)S(1)}, u32[]{:S(2)}, u32[]{:S(2)}) collective-permute-start(f32[16,1,2048]{2,0,1:T(8,128)S(1)} %get-tuple-element.148), channel_id=1, source_target_pairs={{0,4},{4,8},{8,12},{12,16},{16,20},{20,24},{24,28},{28,32},{32,36}... | collective-permute-start | bytes 393224 | tf_op jit(solution)/shard_map/ppermute | solution.py:15
  176.0 12.5 %copy-start.17 = (f32[16,16,2048]{2,0,1:T(8,128)}, f32[16,16,2048]{2,0,1:T(8,128)S(1)}, u32[]{:S(2)}) copy-start(f32[16,16,2048]{2,0,1:T(8,128)S(1)} %get-tuple-element.101) | copy-start | bytes 6291460
  176.0 7.2 %collective-permute-start.13 = (f32[16,1,2048]{2,0,1:T(8,128)S(1)}, f32[16,1,2048]{2,0,1:T(8,128)S(1)}, u32[]{:S(2)}, u32[]{:S(2)}) collective-permute-start(f32[16,1,2048]{2,0,1:T(8,128)S(1)} %get-tuple-element.147), channel_id=1, source_target_pairs={{4,0},{8,4},{12,8},{16,12},{20,16},{24,20},{28,24},{32,28},{36,32}... | collective-permute-start | bytes 393224 | tf_op jit(solution)/shard_map/ppermute | solution.py:18
  180.8 7.7 %collective-permute-start.12 = (f32[16,1,2048]{2,0,1:T(8,128)S(1)}, f32[16,1,2048]{2,0,1:T(8,128)S(1)}, u32[]{:S(2)}, u32[]{:S(2)}) collective-permute-start(f32[16,1,2048]{2,0,1:T(8,128)S(1)} %get-tuple-element.146), channel_id=1, source_target_pairs={{0,4},{4,8},{8,12},{12,16},{16,20},{20,24},{24,28},{28,32},{32,36}... | collective-permute-start | bytes 393224 | tf_op jit(solution)/shard_map/ppermute | solution.py:15
  194.0 7.0 %copy-start.18 = (f32[16,16,2048]{2,0,1:T(8,128)S(1)}, f32[16,16,2048]{2,0,1:T(8,128)}, u32[]{:S(2)}) copy-start(f32[16,16,2048]{2,0,1:T(8,128)} %copy-done.17) | copy-start | bytes 6291460
  194.0 7.0 %copy-start.23 = (f32[16,16,2048]{2,0,1:T(8,128)S(1)}, f32[16,16,2048]{2,0,1:T(8,128)}, u32[]{:S(2)}) copy-start(f32[16,16,2048]{2,0,1:T(8,128)} %copy-done.22) | copy-start | bytes 6291460
  205.5 19.8 %slice-start = ((s8[5242880]{0:T(1024)(128)(4,1)}), s8[4194304]{0:T(1024)(128)(4,1)S(1)}, s32[]{:S(2)}) async-start(s8[5242880]{0:T(1024)(128)(4,1)} %bitcast.113), calls=%async_computation | async-start | bytes 8388608
  212.0 6.7 %copy-start.29 = (f32[32,16,2048]{2,0,1:T(8,128)S(1)}, f32[32,16,2048]{2,0,1:T(8,128)}, u32[]{:S(2)}) copy-start(f32[32,16,2048]{2,0,1:T(8,128)} %get-tuple-element.125) | copy-start | bytes 12582916
  212.0 13.3 %slice-start.1 = ((s8[5242880]{0:T(1024)(128)(4,1)}), s8[1048576]{0:T(1024)(128)(4,1)S(1)}, s32[]{:S(2)}) async-start(s8[5242880]{0:T(1024)(128)(4,1)} %bitcast.113), calls=%async_computation.1 | async-start | bytes 2097152
  221.4 3.8 copy-start.11
  225.3 249.6 %copy-start.1 = (bf16[5,16,16]{2,1,0:T(8,128)(2,1)S(1)}, bf16[5,16,16]{2,1,0:T(8,128)(2,1)}, u32[]{:S(2)}) copy-start(bf16[5,16,16]{2,1,0:T(8,128)(2,1)} %param.25) | copy-start | bytes 7684
  (8 other events, 16.2 us)
where the time goes:
time: 482 us; the launch traced here: 475 us
  blocking collectives  246 us (51%)
  other arithmetic  72.4 us (15%)
  matrix products  57.4 us (12%)
  local copies, waits for them, and re-layouts  39.2 us (8%)
  waiting for transfers between devices  29.6 us (6%)
  starting transfers between devices  28.8 us (6%)
    psum x1, blocking collectives, on_device(): summed = lax.psum(local_sums, 'sky')  246 us
    dot_general x8, matrix products, linked_row(): product = jnp.dot(stacked, matrix, preferred_element_type=jnp.float32)  52.2 us
    add x7, other arithmetic, triple(): return padded[:, :, :-2] + padded[:, :, 1:-1] + padded[:, :, 2:]  41.7 us
    ppermute x8, starting transfers between devices, extended_2(): lax.ppermute(lax.slice_in_dim(block, 0, width, axis=dim), axis, backward)  27.3 us
    ppermute x8, waiting for transfers between devices, extended_2(): lax.ppermute(lax.slice_in_dim(block, block.shape[dim] - width, None, axis...  24.3 us
    slice x4, local copies, waits for them, and re-layouts, stencil(): row_below = extended[:, 2:]  19.1 us
    unnamed x83, local copies, waits for them, and re-layouts  15.2 us
    mul x4, other arithmetic, stencil(): return -0.125 * (vert_above + vert_below + (triple(middle) - middle))  11.1 us
  transfers between devices with their start and end apart: 16, of which 10 were waited for; matrix products, arithmetic and copies ran while one was open for 2% of the time, Pallas kernels for 0%

commit v1 on v0

v1 whole, which is shorter than its diff:
```python
import functools
import math

import jax
import jax.numpy as jnp
from jax import lax
from jax.experimental import pallas as pl
from jax.experimental.pallas import tpu as pltpu
from jax.sharding import PartitionSpec as P

F32 = jnp.float32
BF16 = jnp.bfloat16
LANES = 128
HALO = 4
MESH = pl.DeviceIdType.MESH
CONTRACT_LAST = (((1,), (1,)), ((), ()))


def split_bf16(value):
    high = value.astype(BF16)
    low = (value - high.astype(F32)).astype(BF16)
    return high, low


def remote(source, target, send, recv, peer):
    return pltpu.make_async_remote_copy(
        src_ref=source, dst_ref=target, send_sem=send, recv_sem=recv,
        device_id={"sky": peer}, device_id_type=MESH,
    )


def sweep_row(order, upper, middle, lower, older, link=None, field=None, split=None):
    channels, columns = middle.shape
    blocks = columns // LANES
    lane = lax.broadcasted_iota(jnp.int32, (channels, LANES), 1)
    sums = []
    for block in range(blocks):
        lanes = slice(block * LANES, (block + 1) * LANES)
        value = middle[:, lanes]
        if upper is not None:
            value = value + upper[:, lanes]
        if lower is not None:
            value = value + lower[:, lanes]
        sums.append(value)
    right_moved = [pltpu.roll(value, 1, 1) for value in sums]
    left_moved = [pltpu.roll(value, LANES - 1, 1) for value in sums]
    for block in range(blocks):
        lanes = slice(block * LANES, (block + 1) * LANES)
        from_left = jnp.where(lane == 0, right_moved[block - 1] if block > 0 else 0.0, right_moved[block])
        from_right = jnp.where(
            lane == LANES - 1, left_moved[block + 1] if block < blocks - 1 else 0.0, left_moved[block]
        )
        total = sums[block] + from_left + from_right - middle[:, lanes]
        if link is not None:
            total = total + link[:, lanes]
        if order == 1:
            result = -0.125 * total
        else:
            result = -0.25 * total - older[:, lanes]
        if field is not None:
            field[:, lanes] = result
        if split is not None:
            high, low = split_bf16(result)
            split[channels * order : channels * (order + 1), lanes] = high
            start = channels * (HALO + order)
            split[start : start + channels, lanes] = low


def stacked_weights(weights):
    orders = weights.shape[0]
    return jnp.concatenate(
        [weights[k] for k in range(orders)] + [weights[k] for k in range(1, orders)], axis=1
    )


def block_list(table, homes, slots, which):
    blocks = table.shape[1] // LANES
    for entry in range(3):
        for block in range(blocks):
            homes[entry, block : block + 1, :] = jnp.right_shift(
                table[entry : entry + 1, block * LANES : (block + 1) * LANES], 7
            )
    home = [homes[entry] for entry in range(3)]

    def lowest(candidates):
        least = functools.reduce(jnp.minimum, candidates)
        return jnp.min(least, axis=1, keepdims=True)

    first = lowest(home)
    second = lowest([jnp.where(value > first, value, blocks) for value in home])
    third = lowest([jnp.where(value > second, value, blocks) for value in home])
    lane = lax.broadcasted_iota(jnp.int32, (blocks, LANES), 1)
    more = jnp.max((third < blocks).astype(jnp.int32), axis=0, keepdims=True)
    slots[which] = jnp.where(
        lane == 0,
        jnp.minimum(first, blocks - 1),
        jnp.where(lane == 1, jnp.minimum(second, blocks - 1), more),
    )


def exchange_kernel(
    sky,
    saved, scales, grad, weights, up, down,
    fields, edge_acts, inner_grad, sums, slots, tables,
    flat, acts, split, homes, halo_send, halo_recv, table_send, table_recv,
):
    channels, rows, columns = saved.shape
    orders = weights.shape[0]
    me = lax.axis_index("sky")
    before = lax.rem(me + sky - 1, sky)
    after = lax.rem(me + 1, sky)

    barrier = pltpu.get_barrier_semaphore()
    for peer in (before, after):
        pl.semaphore_signal(barrier, inc=1, device_id={"sky": peer}, device_id_type=MESH)

    for channel in range(channels):
        flat[channel] = grad[channel].astype(F32)
    edge_first = [r for i in range(HALO) for r in (rows - 1 - i, i)]
    for r in edge_first:
        fields[0, HALO + r] = flat[:, r, :]
    pl.semaphore_wait(barrier, 2)

    copies = [
        remote(up.at[0], tables.at[1], table_send.at[0], table_recv.at[0], before),
        remote(down.at[0], tables.at[0], table_send.at[1], table_recv.at[1], after),
    ]
    for i in range(HALO):
        copies += [
            remote(fields.at[0, HALO + i], fields.at[0, HALO + rows + i], halo_send.at[0, i], halo_recv.at[0, i], before),
            remote(fields.at[0, HALO + rows - 1 - i], fields.at[0, HALO - 1 - i], halo_send.at[1, i], halo_recv.at[1, i], after),
        ]
    for copy in copies:
        copy.start()

    for r in range(HALO, rows - HALO):
        value = flat[:, r, :]
        fields[0, HALO + r] = value
        split[r, 0:channels] = value.astype(BF16)

    for order in range(1, orders):
        @pl.loop(order, rows - order, step=2)
        def _(start):
            for r in (start, start + 1):
                row = HALO + r
                sweep_row(
                    order, fields.at[order - 1, row - 1], fields.at[order - 1, row], fields.at[order - 1, row + 1],
                    fields.at[order - 2, row] if order > 1 else None,
                    field=fields.at[order, row] if order < orders - 1 else None, split=split.at[r],
                )

    blocks = scales.shape[2]
    width = columns // blocks

    @pl.loop(0, channels)
    def _(channel):
        scale = scales[channel]
        for block in range(blocks):
            lanes = slice(block * width, (block + 1) * width)
            flat[channel, :, lanes] = saved[channel, :, lanes].astype(F32) * scale[:, block : block + 1]

    for r in range(rows):
        high, low = split_bf16(flat[:, r, :])
        if r < HALO:
            target = edge_acts.at[r]
        elif r >= rows - HALO:
            target = edge_acts.at[r - rows + 2 * HALO]
        else:
            target = acts.at[r - HALO]
        target[0:channels] = high
        target[channels : 2 * channels] = low

    sums[...] = jnp.zeros_like(sums)
    left = stacked_weights(weights)
    for r in range(HALO, rows - HALO):
        sums[...] += lax.dot_general(acts[r - HALO], split[r], CONTRACT_LAST, preferred_element_type=F32)
        inner_grad[r - HALO] = jnp.dot(left, split[r], preferred_element_type=F32)

    block_list(up.at[0], homes, slots, 0)
    block_list(down.at[0], homes, slots, 1)
    for copy in copies[:2]:
        copy.wait()
    block_list(tables.at[0], homes, slots, 2)
    block_list(tables.at[1], homes, slots, 3)
    for copy in copies[2:]:
        copy.wait()


def linked_row(source, table, slots, which, target):
    channels, columns = source.shape
    blocks = columns // LANES

    def source_block(origin):
        return source[:, pl.ds(pl.multiple_of(origin * LANES, LANES), LANES)]

    def indices(out_lanes):
        for entry in range(3):
            index = jnp.broadcast_to(table[entry : entry + 1, out_lanes], (channels, LANES))
            yield jnp.right_shift(index, 7), jnp.bitwise_and(index, LANES - 1)

    def moved(values, lane):
        return jnp.take_along_axis(values, lane, axis=1, mode="promise_in_bounds")

    for block in range(blocks):
        out_lanes = slice(block * LANES, (block + 1) * LANES)
        first, second = slots[which, block, 0], slots[which, block, 1]
        low, high = source_block(first), source_block(second)
        total = None
        for home, lane in indices(out_lanes):
            picked = jnp.where(home == first, moved(low, lane), jnp.where(home == second, moved(high, lane), 0.0))
            total = picked if total is None else total + picked
        target[:, out_lanes] = total

    @pl.when(slots[which, 0, 2] > 0)
    def _():
        @pl.loop(0, blocks)
        def _(block):
            out_lanes = pl.ds(pl.multiple_of(block * LANES, LANES), LANES)

            def add(origin, total):
                values = source_block(origin)
                for home, lane in indices(out_lanes):
                    total = total + jnp.where(home == origin, moved(values, lane), 0.0)
                return total

            target[:, out_lanes] = lax.fori_loop(0, blocks, add, jnp.zeros((channels, LANES), F32))


def edge_kernel(
    fields, edge_acts, inner_grad, inner_sums, slots, tables, up, down, weights,
    out, local,
    fresh, split, links, flat,
):
    channels, rows, columns = out.shape
    orders = weights.shape[0]
    top = HALO
    bottom = HALO + rows - 1
    mirror = 2 * HALO + rows - 1

    def edge(r):
        return r if r < HALO else r - rows + 2 * HALO

    def field(order, row):
        if order == 0 or HALO + order <= row <= bottom - order:
            return fields.at[order, row]
        at = row - order if row <= HALO + order else HALO + row - (mirror - HALO - order + 1)
        return fresh.at[order - 1, at]

    for r in range(HALO, rows - HALO):
        flat[:, r, :] = inner_grad[r - HALO]
    for r in list(range(HALO)) + list(range(rows - HALO, rows)):
        depth = min(r, rows - 1 - r)
        split[edge(r), 0:channels] = fields[0, HALO + r].astype(BF16)
        for order in range(1, depth + 1):
            high, low = split_bf16(fields[order, HALO + r])
            split[edge(r), channels * order : channels * (order + 1)] = high
            split[edge(r), channels * (HALO + order) : channels * (HALO + order + 1)] = low

    for order in range(1, orders):
        last = order == orders - 1
        linked_row(field(order - 1, top - 1), up.at[0], slots, 0, links.at[0])
        linked_row(field(order - 1, bottom + 1), down.at[0], slots, 1, links.at[1])
        if not last:
            linked_row(field(order - 1, top), tables.at[0], slots, 2, links.at[2])
            linked_row(field(order - 1, bottom), tables.at[1], slots, 3, links.at[3])
        for near in range(order, HALO + order):
            for row in (near, mirror - near):
                upper, lower, link = field(order - 1, row - 1), field(order - 1, row + 1), None
                if row == top:
                    upper, link = None, links.at[0]
                elif row == bottom:
                    lower, link = None, links.at[1]
                elif row == top - 1:
                    lower, link = None, links.at[2]
                elif row == bottom + 1:
                    upper, link = None, links.at[3]
                sweep_row(
                    order, upper, field(order - 1, row), lower, field(order - 2, row) if order > 1 else None,
                    link=link, field=None if last else field(order, row),
                    split=split.at[edge(row - HALO)] if top <= row <= bottom else None,
                )

    sums = inner_sums[...]
    for r in range(2 * HALO):
        sums += lax.dot_general(edge_acts[r], split[r], CONTRACT_LAST, preferred_element_type=F32)
    lane = lax.broadcasted_iota(jnp.int32, (channels, LANES), 1)
    both = sums[0:channels] + sums[channels : 2 * channels]
    first = both[:, 0:LANES]
    second = jnp.concatenate([both[:, LANES:], jnp.zeros((channels, 2 * LANES - both.shape[1]), F32)], axis=1)
    moved = jnp.where(lane < LANES // 2, pltpu.roll(first, LANES // 2, 1), pltpu.roll(second, LANES // 2, 1))
    wide = channels * orders
    local[...] = jnp.where(lane < wide, first, 0.0) + jnp.where((lane >= channels) & (lane < wide), moved, 0.0)

    left = stacked_weights(weights)
    for r in list(range(HALO)) + list(range(rows - HALO, rows)):
        flat[:, r, :] = jnp.dot(left, split[edge(r)], preferred_element_type=F32)
    for channel in range(channels):
        out[channel] = flat[channel].astype(BF16)


def sum_kernel(sky, inner, norm, local, weight_grad, part_in, part_out, in_send, in_recv, out_send, out_recv):
    orders, channels = weight_grad.shape[:2]
    outer = sky // inner
    me = lax.axis_index("sky")
    slot = lax.rem(me, inner)
    group = lax.div(me, inner)

    def in_peer(step):
        return group * inner + lax.rem(slot + step, inner)

    def out_peer(step):
        return lax.rem(group + step, outer) * inner + slot

    barrier = pltpu.get_barrier_semaphore()
    peers = [in_peer(step) for step in range(1, inner)] + [out_peer(step) for step in range(1, outer)]
    for peer in peers:
        pl.semaphore_signal(barrier, inc=1, device_id={"sky": peer}, device_id_type=MESH)
    part_in[slot] = local[...]
    pl.semaphore_wait(barrier, len(peers))

    def exchange(buffer, own, count, peer_of, send, recv):
        copies = [
            remote(buffer.at[own], buffer.at[own], send.at[step], recv.at[step], peer_of(step))
            for step in range(1, count)
        ]
        for copy in copies:
            copy.start()
        for copy in copies:
            copy.wait()
        return functools.reduce(lambda total, i: total + buffer[i], range(1, count), buffer[0])

    part_out[group] = exchange(part_in, slot, inner, in_peer, in_send, in_recv)
    total = exchange(part_out, group, outer, out_peer, out_send, out_recv) * norm
    for k in range(orders):
        weight_grad[k] = total[:, channels * k : channels * (k + 1)]


def on_device(sky, saved_acts, scales, grad_out, weights, edge_up, edge_down):
    channels, rows, columns = saved_acts.shape
    orders = weights.shape[0]
    inner = min(8, sky)
    outer = sky // inner
    norm = 1.0 / math.sqrt(rows * columns * sky)
    stacked = channels * (2 * orders - 1)
    vmem = pl.BlockSpec(memory_space=pltpu.VMEM)
    smem = pl.BlockSpec(memory_space=pltpu.SMEM)
    dma = pltpu.SemaphoreType.DMA
    shape = jax.ShapeDtypeStruct
    fields, edge_acts, inner_grad, sums, slots, tables = pl.pallas_call(
        functools.partial(exchange_kernel, sky),
        out_shape=(
            shape((orders - 1, rows + 2 * HALO, channels, columns), F32),
            shape((2 * HALO, 2 * channels, columns), BF16),
            shape((rows - 2 * HALO, channels, columns), F32),
            shape((2 * channels, stacked), F32),
            shape((4, columns // LANES, LANES), jnp.int32),
            shape((2, 3, columns), jnp.int32),
        ),
        in_specs=[vmem] * 6,
        out_specs=(vmem,) * 6,
        scratch_shapes=[
            pltpu.VMEM((channels, rows, columns), F32),
            pltpu.VMEM((rows - 2 * HALO, 2 * channels, columns), BF16),
            pltpu.VMEM((rows, stacked, columns), BF16),
            pltpu.VMEM((3, columns // LANES, LANES), jnp.int32),
            dma((2, HALO)), dma((2, HALO)), dma((2,)), dma((2,)),
        ],
        compiler_params=pltpu.CompilerParams(
            collective_id=0, has_side_effects=True, vmem_limit_bytes=32 * 2**20
        ),
        name="exchange",
    )(saved_acts, scales, grad_out, weights, edge_up, edge_down)
    grad_in, local = pl.pallas_call(
        edge_kernel,
        out_shape=(shape((channels, rows, columns), BF16), shape((channels, LANES), F32)),
        in_specs=[vmem] * 4 + [smem] + [vmem] * 4,
        out_specs=(vmem, vmem),
        scratch_shapes=[
            pltpu.VMEM((orders - 2, 2 * HALO, channels, columns), F32),
            pltpu.VMEM((2 * HALO, stacked, columns), BF16),
            pltpu.VMEM((4, channels, columns), F32),
            pltpu.VMEM((channels, rows, columns), F32),
        ],
        compiler_params=pltpu.CompilerParams(vmem_limit_bytes=32 * 2**20),
        name="edges",
    )(fields, edge_acts, inner_grad, sums, slots, tables, edge_up, edge_down, weights)
    weight_grad = pl.pallas_call(
        functools.partial(sum_kernel, sky, inner, norm),
        out_shape=shape((orders, channels, channels), F32),
        in_specs=[vmem],
        out_specs=vmem,
        scratch_shapes=[
            pltpu.VMEM((inner, channels, LANES), F32),
            pltpu.VMEM((outer, channels, LANES), F32),
            dma((inner,)), dma((inner,)), dma((outer,)), dma((outer,)),
        ],
        compiler_params=pltpu.CompilerParams(collective_id=1, has_side_effects=True),
        name="sky_sum",
    )(local)
    return grad_in, weight_grad


def solution(mesh):
    return jax.shard_map(
        functools.partial(on_device, mesh.shape["sky"]),
        mesh=mesh,
        in_specs=(
            P("rep", "sky", None),
            P("rep", "sky", None),
            P("rep", "sky", None),
            P(),
            P("sky", None, None),
            P("sky", None, None),
        ),
        out_specs=(P("rep", "sky", None), P("rep", None, None)),
        check_vma=False,
    )
```

time: 482 us -> 206 us (0.43); the launches traced: 475 us -> 204 us
  blocking collectives: 246 us -> 0 us
  Pallas kernels: 0 us -> 196 us
  other arithmetic: 72.4 us -> 0 us
  matrix products: 57.4 us -> 0 us
  local copies, waits for them, and re-layouts: 39.2 us -> 7.58 us
  waiting for transfers between devices: 29.6 us -> 0 us
  starting transfers between devices: 28.8 us -> 0 us
    psum x1 -> x0, blocking collectives: 246 us -> none  [on_device(): summed = lax.psum(local_sums, 'sky')]
    pallas_call x0 -> x3, Pallas kernels: none -> 196 us  [the longest x1 158 us: on_device(): pl.pallas_call(functools.partial(sum_kernel, sky, inner, norm), out_shape...]
    dot_general x10 -> x0, matrix products: 57.4 us -> none  [the longest x8 52.2 us: linked_row(): product = jnp.dot(stacked, matrix, preferred_element_type=jnp.float32)]
    add x7 -> x0, other arithmetic: 41.7 us -> none  [triple(): return padded[:, :, :-2] + padded[:, :, 1:-1] + padded[:, :, 2:]]
    ppermute x16 -> x0, waiting for transfers between devices: 29.6 us -> none  [the longest x8 24.3 us: extended_2(): lax.ppermute(lax.slice_in_dim(block, block.shape[dim] - width, None, axis...]
    ppermute x16 -> x0, starting transfers between devices: 28.8 us -> none  [the longest x8 27.3 us: extended_2(): lax.ppermute(lax.slice_in_dim(block, 0, width, axis=dim), axis, backward)]
    slice x14 -> x0, local copies, waits for them, and re-layouts: 20 us -> none  [the longest x4 19.1 us: stencil(): row_below = extended[:, 2:]]
    mul x5 -> x0, other arithmetic: 11.7 us -> none  [the longest x4 11.1 us: stencil(): return -0.125 * (vert_above + vert_below + (triple(middle) - middle))]
  transfers between devices with their start and end apart: 16 -> 0, of which waited for: 10 -> 0; matrix products, arithmetic and copies ran while one was open for 2% -> 0% of each run, Pallas kernels for 0% -> 0%
where the time goes in v1:
time: 206 us; the launch traced here: 204 us
  Pallas kernels  196 us (95%)
  local copies, waits for them, and re-layouts  7.58 us (4%)
    pallas_call x1, Pallas kernels, on_device(): pl.pallas_call(functools.partial(sum_kernel, sky, inner, norm), out_shape...  158 us
    pallas_call x1, Pallas kernels, on_device(): pl.pallas_call(functools.partial(exchange_kernel, sky), out_shape=(shape(...  25.6 us
    pallas_call x1, Pallas kernels, on_device(): pl.pallas_call(edge_kernel, out_shape=(shape((channels, rows, columns), B...  12.9 us
    unnamed x13, local copies, waits for them, and re-layouts  7.58 us

profile of v1, /device:TPU:4, one launch (start us, length us, event | category | flops | bytes accessed | tf_op | source)
XLA Modules:
  0.0 204.5 jit_solution(14842821226756784713)
XLA Ops:
  0.6 0.8 copy.8.up
  1.4 0.8 copy.9.down
  2.1 0.0 copy-start
  2.2 1.2 copy-done
  3.4 0.0 copy-start.1
  3.4 1.2 copy-done.1
  4.6 0.0 copy-start.2
  4.6 0.9 copy-done.2
  5.5 0.0 copy-start.3
  5.5 0.7 copy-done.3
  6.2 25.6 %exchange.1 = (f32[4,24,16,2048]{3,2,1,0:T(8,128)S(1)}, bf16[8,32,2048]{2,1,0:T(8,128)(2,1)S(1)}, f32[8,16,2048]{2,1,0:T(8,128)S(1)}, f32[32,144]{1,0:T(8,128)S(...) custom-call(bf16[16,16,2048]{2,1,0:T(8,128)(2,1)S(1)} %copy-done, f32[16,16,16]{2,1,0:T(8,128)S(1)} %copy-done.2, ...), custom_call_target="tpu_custom_call" | custom-call | tf_op jit(solution)/shard_map/exchange/pallas_call | solution.py:349
  31.8 12.9 %edges.1 = (bf16[16,16,2048]{2,1,0:T(8,128)(2,1)}, f32[16,128]{1,0:T(8,128)S(1)}) custom-call(f32[4,24,16,2048]{3,2,1,0:T(8,128)S(1)} %get-tuple-element.10.fields, bf16[8,32,2048]{2,1,0:T(8,128)(2,1)S(1)} %get-tuple-element.11.edge_acts, f32[8,16,2048]{2,1,0:T(8,128)S(1)} %get-tuple-element.12.inner_grad, f32[32,144]{1,0:T(8,128)S(1)} %get-tuple-element.13.inner_sums, ...), custom_call_target="tpu_custom_call" | custom-call | tf_op jit(solution)/shard_map/edges/pallas_call | solution.py:373
  44.8 0.0 copy-start.4
  44.8 0.6 copy-done.4
  45.3 157.7 %sky_sum.1 = f32[5,16,16]{2,1,0:T(8,128)} custom-call(f32[16,128]{1,0:T(8,128)} %copy-done.4), custom_call_target="tpu_custom_call" | custom-call | tf_op jit(solution)/shard_map/sky_sum/pallas_call | solution.py:387
  203.1 1.4 copy.13
Async XLA Ops:
  2.1 1.2 copy-start
  3.4 1.2 copy-start.1
  4.6 0.9 copy-start.2
  5.5 0.7 copy-start.3
  44.8 0.6 copy-start.4

commit v2 on v1

v2 whole, which is shorter than its diff:
```python
import functools
import math

import jax
import jax.numpy as jnp
from jax import lax
from jax.experimental import pallas as pl
from jax.experimental.pallas import tpu as pltpu
from jax.sharding import PartitionSpec as P

F32 = jnp.float32
BF16 = jnp.bfloat16
LANES = 128
HALO = 4
MESH = pl.DeviceIdType.MESH
CONTRACT_LAST = (((1,), (1,)), ((), ()))


def split_bf16(value):
    high = value.astype(BF16)
    low = (value - high.astype(F32)).astype(BF16)
    return high, low


def remote(source, target, send, recv, peer):
    return pltpu.make_async_remote_copy(
        src_ref=source, dst_ref=target, send_sem=send, recv_sem=recv,
        device_id={"sky": peer}, device_id_type=MESH,
    )


def sweep_row(order, upper, middle, lower, older, link=None, field=None, split=None):
    channels, columns = middle.shape
    blocks = columns // LANES
    lane = lax.broadcasted_iota(jnp.int32, (channels, LANES), 1)
    sums = []
    for block in range(blocks):
        lanes = slice(block * LANES, (block + 1) * LANES)
        value = middle[:, lanes]
        if upper is not None:
            value = value + upper[:, lanes]
        if lower is not None:
            value = value + lower[:, lanes]
        sums.append(value)
    right_moved = [pltpu.roll(value, 1, 1) for value in sums]
    left_moved = [pltpu.roll(value, LANES - 1, 1) for value in sums]
    for block in range(blocks):
        lanes = slice(block * LANES, (block + 1) * LANES)
        from_left = jnp.where(lane == 0, right_moved[block - 1] if block > 0 else 0.0, right_moved[block])
        from_right = jnp.where(
            lane == LANES - 1, left_moved[block + 1] if block < blocks - 1 else 0.0, left_moved[block]
        )
        total = sums[block] + from_left + from_right - middle[:, lanes]
        if link is not None:
            total = total + link[:, lanes]
        if order == 1:
            result = -0.125 * total
        else:
            result = -0.25 * total - older[:, lanes]
        if field is not None:
            field[:, lanes] = result
        if split is not None:
            high, low = split_bf16(result)
            split[channels * order : channels * (order + 1), lanes] = high
            start = channels * (HALO + order)
            split[start : start + channels, lanes] = low


def stacked_weights(weights):
    orders = weights.shape[0]
    return jnp.concatenate(
        [weights[k] for k in range(orders)] + [weights[k] for k in range(1, orders)], axis=1
    )


def block_list(table, homes, slots, which):
    blocks = table.shape[-1] // LANES
    for entry in range(3):
        for block in range(blocks):
            homes[entry, block : block + 1, :] = jnp.right_shift(
                table[entry, :, block * LANES : (block + 1) * LANES], 7
            )
    lane = lax.broadcasted_iota(jnp.int32, (blocks, LANES), 1)
    packed = jnp.zeros((blocks, LANES), jnp.int32)
    more = jnp.zeros((blocks, 1), jnp.int32)
    for entry in range(3):
        home = homes[entry]
        first = jnp.min(home, axis=1, keepdims=True)
        second = jnp.min(jnp.where(home > first, home, blocks), axis=1, keepdims=True)
        third = jnp.min(jnp.where(home > second, home, blocks), axis=1, keepdims=True)
        packed = jnp.where(lane == entry, jnp.minimum(first, blocks - 1), packed)
        packed = jnp.where(lane == 3 + entry, jnp.minimum(second, blocks - 1), packed)
        more = jnp.maximum(more, (third < blocks).astype(jnp.int32))
    slots[which] = jnp.where(lane == 6, jnp.max(more, axis=0, keepdims=True), packed)


def exchange_kernel(
    sky,
    saved_hbm, scales_hbm, grad_hbm, weights_hbm, up_hbm, down_hbm,
    fields, split, acts, sums, slots, tables, left,
    saved, scales, grad, weights, flat, rows_x, scale_rows, homes,
    halo_send, halo_recv, table_send, table_recv, load,
):
    channels, rows, columns = saved.shape
    orders = weights.shape[0]
    blocks = scales.shape[2]
    width = columns // blocks
    me = lax.axis_index("sky")
    before = lax.rem(me + sky - 1, sky)
    after = lax.rem(me + 1, sky)

    barrier = pltpu.get_barrier_semaphore()
    for peer in (before, after):
        pl.semaphore_signal(barrier, inc=1, device_id={"sky": peer}, device_id_type=MESH)
    loads = [
        pltpu.make_async_copy(source, target, load.at[i])
        for i, (source, target) in enumerate(
            [
                (grad_hbm, grad),
                (up_hbm, tables.at[0]),
                (down_hbm, tables.at[1]),
                (saved_hbm, saved),
                (scales_hbm, scales),
                (weights_hbm, weights),
            ]
        )
    ]
    for copy in loads:
        copy.start()

    loads[0].wait()
    for channel in range(channels):
        flat[channel] = grad[channel].astype(F32)
    edge_first = [r for i in range(HALO) for r in (rows - 1 - i, i)]
    for r in edge_first:
        fields[0, HALO + r] = flat[:, r, :]
    loads[1].wait()
    loads[2].wait()
    pl.semaphore_wait(barrier, 2)

    copies = []
    for i in range(HALO):
        copies += [
            remote(fields.at[0, HALO + i], fields.at[0, HALO + rows + i], halo_send.at[0, i], halo_recv.at[0, i], before),
            remote(fields.at[0, HALO + rows - 1 - i], fields.at[0, HALO - 1 - i], halo_send.at[1, i], halo_recv.at[1, i], after),
        ]
    copies += [
        remote(tables.at[0], tables.at[3], table_send.at[0], table_recv.at[0], before),
        remote(tables.at[1], tables.at[2], table_send.at[1], table_recv.at[1], after),
    ]
    for copy in copies:
        copy.start()

    for r in range(HALO, rows - HALO):
        fields[0, HALO + r] = flat[:, r, :]

    @pl.loop(0, rows)
    def _(r):
        split[r, 0:channels] = fields[0, HALO + r].astype(BF16)

    for order in range(1, orders):
        @pl.loop(order, rows - order, step=2)
        def _(start):
            for r in (start, start + 1):
                row = HALO + r
                sweep_row(
                    order, fields.at[order - 1, row - 1], fields.at[order - 1, row], fields.at[order - 1, row + 1],
                    fields.at[order - 2, row] if order > 1 else None,
                    field=fields.at[order, row] if order < orders - 1 else None, split=split.at[r],
                )

    for copy in loads[3:]:
        copy.wait()
    for channel in range(channels):
        flat[channel] = saved[channel].astype(F32)
    for r in range(rows):
        rows_x[r] = flat[:, r, :]
        scale_rows[r] = scales[:, r, :]

    @pl.loop(0, rows)
    def _(r):
        for block in range(blocks):
            lanes = slice(block * width, (block + 1) * width)
            high, low = split_bf16(rows_x[r, :, lanes] * scale_rows[r, :, block : block + 1])
            acts[r, 0:channels, lanes] = high
            acts[r, channels : 2 * channels, lanes] = low

    left[...] = stacked_weights(weights)
    sums[...] = jnp.zeros_like(sums)
    for r in range(HALO, rows - HALO):
        sums[...] += lax.dot_general(acts[r], split[r], CONTRACT_LAST, preferred_element_type=F32)

    block_list(tables.at[0], homes, slots, 0)
    block_list(tables.at[1], homes, slots, 1)
    for copy in copies[2 * HALO :]:
        copy.wait()
    block_list(tables.at[2], homes, slots, 2)
    block_list(tables.at[3], homes, slots, 3)
    for copy in copies[: 2 * HALO]:
        copy.wait()


def linked_row(source, table, slots, which, target):
    channels, columns = source.shape
    blocks = columns // LANES

    def source_block(origin):
        return source[:, pl.ds(pl.multiple_of(origin * LANES, LANES), LANES)]

    def indices(entry, out_lanes):
        index = jnp.broadcast_to(table[entry, :, out_lanes], (channels, LANES))
        return jnp.right_shift(index, 7), jnp.bitwise_and(index, LANES - 1)

    def moved(values, lane):
        return jnp.take_along_axis(values, lane, axis=1, mode="promise_in_bounds")

    for block in range(blocks):
        out_lanes = slice(block * LANES, (block + 1) * LANES)
        total = None
        for entry in range(3):
            first, second = slots[which, block, entry], slots[which, block, 3 + entry]
            home, lane = indices(entry, out_lanes)
            picked = jnp.where(
                home == first,
                moved(source_block(first), lane),
                jnp.where(home == second, moved(source_block(second), lane), 0.0),
            )
            total = picked if total is None else total + picked
        target[:, out_lanes] = total

    @pl.when(slots[which, 0, 6] > 0)
    def _():
        @pl.loop(0, blocks)
        def _(block):
            out_lanes = pl.ds(pl.multiple_of(block * LANES, LANES), LANES)

            def add(origin, total):
                values = source_block(origin)
                for entry in range(3):
                    home, lane = indices(entry, out_lanes)
                    total = total + jnp.where(home == origin, moved(values, lane), 0.0)
                return total

            target[:, out_lanes] = lax.fori_loop(0, blocks, add, jnp.zeros((channels, LANES), F32))


def edge_kernel(fields, inner_split, slots, tables, split, fresh, links):
    rows = inner_split.shape[0]
    channels = fields.shape[2]
    orders = fields.shape[0] + 1
    top = HALO
    bottom = HALO + rows - 1
    mirror = 2 * HALO + rows - 1

    def field(order, row):
        if order == 0 or HALO + order <= row <= bottom - order:
            return fields.at[order, row]
        at = row - order if row <= HALO + order else HALO + row - (mirror - HALO - order + 1)
        return fresh.at[order - 1, at]

    def edge(r):
        return r if r < HALO else r - rows + 2 * HALO

    for r in range(HALO):
        for row in (r, rows - 1 - r):
            known = slice(0, channels * (r + 1))
            split[edge(row), known] = inner_split[row, known]
            if r > 0:
                known = slice(channels * (HALO + 1), channels * (HALO + 1 + r))
                split[edge(row), known] = inner_split[row, known]

    for order in range(1, orders):
        last = order == orders - 1
        linked_row(field(order - 1, top - 1), tables.at[0], slots, 0, links.at[0])
        linked_row(field(order - 1, bottom + 1), tables.at[1], slots, 1, links.at[1])
        if not last:
            linked_row(field(order - 1, top), tables.at[2], slots, 2, links.at[2])
            linked_row(field(order - 1, bottom), tables.at[3], slots, 3, links.at[3])
        for near in range(order, HALO + order):
            for row in (near, mirror - near):
                upper, lower, link = field(order - 1, row - 1), field(order - 1, row + 1), None
                if row == top:
                    upper, link = None, links.at[0]
                elif row == bottom:
                    lower, link = None, links.at[1]
                elif row == top - 1:
                    lower, link = None, links.at[2]
                elif row == bottom + 1:
                    upper, link = None, links.at[3]
                sweep_row(
                    order, upper, field(order - 1, row), lower, field(order - 2, row) if order > 1 else None,
                    link=link, field=None if last else field(order, row),
                    split=split.at[edge(row - HALO)] if top <= row <= bottom else None,
                )


def sum_kernel(
    sky, inner, norm,
    split, edge_split, acts, inner_sums, left,
    out, weight_grad,
    flat, part_in, part_out, in_send, in_recv, out_send, out_recv,
):
    channels, rows, columns = out.shape
    orders = weight_grad.shape[0]
    outer = sky // inner
    me = lax.axis_index("sky")
    slot = lax.rem(me, inner)
    group = lax.div(me, inner)

    def in_peer(step):
        return group * inner + lax.rem(slot + step, inner)

    def out_peer(step):
        return lax.rem(group + step, outer) * inner + slot

    barrier = pltpu.get_barrier_semaphore()
    peers = [in_peer(step) for step in range(1, inner)] + [out_peer(step) for step in range(1, outer)]
    for peer in peers:
        pl.semaphore_signal(barrier, inc=1, device_id={"sky": peer}, device_id_type=MESH)

    def terms(r):
        if r < HALO:
            return edge_split[r]
        return split[r] if r < rows - HALO else edge_split[r - rows + 2 * HALO]

    sums = inner_sums[...]
    for r in list(range(HALO)) + list(range(rows - HALO, rows)):
        sums += lax.dot_general(acts[r], terms(r), CONTRACT_LAST, preferred_element_type=F32)
    lane = lax.broadcasted_iota(jnp.int32, (channels, LANES), 1)
    both = sums[0:channels] + sums[channels : 2 * channels]
    first = both[:, 0:LANES]
    second = jnp.concatenate([both[:, LANES:], jnp.zeros((channels, 2 * LANES - both.shape[1]), F32)], axis=1)
    moved = jnp.where(lane < LANES // 2, pltpu.roll(first, LANES // 2, 1), pltpu.roll(second, LANES // 2, 1))
    wide = channels * orders
    part_in[slot] = jnp.where(lane < wide, first, 0.0) + jnp.where((lane >= channels) & (lane < wide), moved, 0.0)
    pl.semaphore_wait(barrier, len(peers))

    def exchange(buffer, own, count, peer_of, send, recv):
        copies = [
            remote(buffer.at[own], buffer.at[own], send.at[step], recv.at[step], peer_of(step))
            for step in range(1, count)
        ]
        for copy in copies:
            copy.start()
        return copies

    def total_of(buffer, copies):
        for copy in copies:
            copy.wait()
        return functools.reduce(lambda total, i: total + buffer[i], range(1, len(copies) + 1), buffer[0])

    copies = exchange(part_in, slot, inner, in_peer, in_send, in_recv)
    for r in range(rows):
        flat[:, r, :] = jnp.dot(left[...], terms(r), preferred_element_type=F32)
    part_out[group] = total_of(part_in, copies)
    copies = exchange(part_out, group, outer, out_peer, out_send, out_recv)
    for channel in range(channels):
        out[channel] = flat[channel].astype(BF16)
    total = total_of(part_out, copies) * norm
    for k in range(orders):
        weight_grad[k] = total[:, channels * k : channels * (k + 1)]


def on_device(sky, saved_acts, scales, grad_out, weights, edge_up, edge_down):
    channels, rows, columns = saved_acts.shape
    orders = weights.shape[0]
    blocks = scales.shape[2]
    inner = min(8, sky)
    outer = sky // inner
    norm = 1.0 / math.sqrt(rows * columns * sky)
    stacked = channels * (2 * orders - 1)
    vmem = pl.BlockSpec(memory_space=pltpu.VMEM)
    smem = pl.BlockSpec(memory_space=pltpu.SMEM)
    hbm = pl.BlockSpec(memory_space=pltpu.HBM)
    dma = pltpu.SemaphoreType.DMA
    shape = jax.ShapeDtypeStruct
    up, down = jnp.transpose(edge_up, (1, 0, 2)), jnp.transpose(edge_down, (1, 0, 2))
    fields, split, acts, sums, slots, tables, left = pl.pallas_call(
        functools.partial(exchange_kernel, sky),
        out_shape=(
            shape((orders - 1, rows + 2 * HALO, channels, columns), F32),
            shape((rows, stacked, columns), BF16),
            shape((rows, 2 * channels, columns), BF16),
            shape((2 * channels, stacked), F32),
            shape((4, columns // LANES, LANES), jnp.int32),
            shape((4, 3, 1, columns), jnp.int32),
            shape((channels, stacked), BF16),
        ),
        in_specs=[hbm] * 6,
        out_specs=(vmem,) * 7,
        scratch_shapes=[
            pltpu.VMEM((channels, rows, columns), BF16),
            pltpu.VMEM((channels, rows, blocks), F32),
            pltpu.VMEM((channels, rows, columns), BF16),
            pltpu.VMEM((orders, channels, channels), BF16),
            pltpu.VMEM((channels, rows, columns), F32),
            pltpu.VMEM((rows, channels, columns), F32),
            pltpu.VMEM((rows, channels, blocks), F32),
            pltpu.VMEM((3, columns // LANES, LANES), jnp.int32),
            dma((2, HALO)), dma((2, HALO)), dma((2,)), dma((2,)), dma((6,)),
        ],
        compiler_params=pltpu.CompilerParams(
            collective_id=0, has_side_effects=True, vmem_limit_bytes=12 * 2**20
        ),
        name="exchange",
    )(*(pltpu.with_memory_space_constraint(x, pltpu.HBM) for x in (saved_acts, scales, grad_out, weights, up, down)))
    edge_split = pl.pallas_call(
        edge_kernel,
        out_shape=shape((2 * HALO, stacked, columns), BF16),
        in_specs=[vmem, vmem, smem, vmem],
        out_specs=vmem,
        scratch_shapes=[
            pltpu.VMEM((orders - 2, 2 * HALO, channels, columns), F32),
            pltpu.VMEM((4, channels, columns), F32),
        ],
        compiler_params=pltpu.CompilerParams(vmem_limit_bytes=12 * 2**20),
        name="edges",
    )(fields, split, slots, tables)
    return pl.pallas_call(
        functools.partial(sum_kernel, sky, inner, norm),
        out_shape=(shape((channels, rows, columns), BF16), shape((orders, channels, channels), F32)),
        in_specs=[vmem] * 5,
        out_specs=(vmem, vmem),
        scratch_shapes=[
            pltpu.VMEM((channels, rows, columns), F32),
            pltpu.VMEM((inner, channels, LANES), F32),
            pltpu.VMEM((outer, channels, LANES), F32),
            dma((inner,)), dma((inner,)), dma((outer,)), dma((outer,)),
        ],
        compiler_params=pltpu.CompilerParams(
            collective_id=1, has_side_effects=True, vmem_limit_bytes=12 * 2**20
        ),
        name="sky_sum",
    )(split, edge_split, acts, sums, left)


def solution(mesh):
    return jax.shard_map(
        functools.partial(on_device, mesh.shape["sky"]),
        mesh=mesh,
        in_specs=(
            P("rep", "sky", None),
            P("rep", "sky", None),
            P("rep", "sky", None),
            P(),
            P("sky", None, None),
            P("sky", None, None),
        ),
        out_specs=(P("rep", "sky", None), P("rep", None, None)),
        check_vma=False,
    )
```

time: 206 us -> 42.3 us (0.21)
  Pallas kernels: 196 us -> 39.7 us
  local copies, waits for them, and re-layouts: 7.58 us -> 1.59 us
    pallas_call x1, Pallas kernels: 158 us -> 11.3 us  [on_device(): pl.pallas_call(functools.partial(sum_kernel, sky, inner, norm), out_shape...]
    pallas_call x1, Pallas kernels: 25.6 us -> 18.5 us  [on_device(): pl.pallas_call(functools.partial(exchange_kernel, sky), out_shape=(shape(...]
    unnamed x13 -> x2, local copies, waits for them, and re-layouts: 7.58 us -> 1.59 us
    pallas_call x1, Pallas kernels: 12.9 us -> 9.87 us  [on_device(): pl.pallas_call(edge_kernel, out_shape=shape((2 * HALO, stacked, columns),...]
where the time goes in v2:
time: 42.3 us; the launch traced here: 41.9 us
  Pallas kernels  39.7 us (94%)
  local copies, waits for them, and re-layouts  1.59 us (4%)
  between operations  0.65 us (2%)
    pallas_call x1, Pallas kernels, on_device(): pl.pallas_call(functools.partial(exchange_kernel, sky), out_shape=(shape(...  18.5 us
    pallas_call x1, Pallas kernels, on_device(): pl.pallas_call(functools.partial(sum_kernel, sky, inner, norm), out_shape...  11.3 us
    pallas_call x1, Pallas kernels, on_device(): pl.pallas_call(edge_kernel, out_shape=shape((2 * HALO, stacked, columns),...  9.87 us
    unnamed x2, local copies, waits for them, and re-layouts  1.59 us

profile of v2, /device:TPU:4, one launch (start us, length us, event | category | flops | bytes accessed | tf_op | source)
XLA Modules:
  0.0 41.9 jit_solution(16961842446209316854)
XLA Ops:
  0.6 18.5 %exchange.1 = (f32[4,24,16,2048]{3,2,1,0:T(8,128)S(1)}, bf16[16,144,2048]{2,1,0:T(8,128)(2,1)S(1)}, bf16[16,32,2048]{2,1,0:T(8,128)(2,1)S(1)}, f32[32,144]{1,0:T...) custom-call(bf16[16,16,2048]{2,1,0:T(8,128)(2,1)} %saved_hbm.1, ...), custom_call_target="tpu_custom_call" | custom-call | tf_op jit(solution)/shard_map/exchange/pallas_call | solution.py:378
  19.1 9.9 %edges.1.edge_split = bf16[8,144,2048]{2,1,0:T(8,128)(2,1)S(1)} custom-call(f32[4,24,16,2048]{3,2,1,0:T(8,128)S(1)} %get-tuple-element.10.fields, bf16[16,144,2048]{2,1,0:T(8,128)(2,1)S(1)} %get-tuple-element.9.inner_split.split, s32[4,16,128]{2,1,0:T(8,128)S(1)} %get-tuple-element.11.slots, s32[4,3,1,2048]{3,2,1,0:T(1,128)S(1)} %get-tuple-element.12.tables), custom_call_target="tpu_custom_call" | custom-call | tf_op jit(solution)/shard_map/edges/pallas_call | solution.py:407
  29.0 11.3 %sky_sum.1 = (bf16[16,16,2048]{2,1,0:T(8,128)(2,1)S(1)}, f32[5,16,16]{2,1,0:T(8,128)S(1)}) custom-call(bf16[16,144,2048]{2,1,0:T(8,128)(2,1)S(1)} %get-tuple-element.9.inner_split.split, bf16[8,144,2048]{2,1,0:T(8,128)(2,1)S(1)} %edges.1.edge_split, bf16[16,32,2048]{2,1,0:T(8,128)(2,1)S(1)} %get-tuple-element.13.acts, ...), custom_call_target="tpu_custom_call" | custom-call | tf_op jit(solution)/shard_map/sky_sum/pallas_call | solution.py:419
  40.4 1.0 %copy.10 = bf16[16,16,2048]{2,1,0:T(8,128)(2,1)} copy(bf16[16,16,2048]{2,1,0:T(8,128)(2,1)S(1)} %get-tuple-element.18) | data formatting | bytes 2097152
  41.3 0.6 %copy.11 = f32[5,16,16]{2,1,0:T(8,128)} copy(f32[5,16,16]{2,1,0:T(8,128)S(1)} %get-tuple-element.19) | data formatting | bytes 10240

commit v3 on v2

--- a/solution.py
+++ b/solution.py
@@ -14,6 +14,12 @@
 HALO = 4
 MESH = pl.DeviceIdType.MESH
 CONTRACT_LAST = (((1,), (1,)), ((), ()))
+TERMS = ((0, 0), (1, 0), (2, 0), (2, 1), (3, 0), (3, 1), (4, 0), (4, 1))
+LEVELS = 10922.0
+GATHER = lax.GatherDimensionNumbers(
+    offset_dims=(), collapsed_slice_dims=(1,), start_index_map=(1,),
+    operand_batching_dims=(0,), start_indices_batching_dims=(0,),
+)
 
 
 def split_bf16(value):
@@ -60,17 +66,17 @@
         if field is not None:
             field[:, lanes] = result
         if split is not None:
-            high, low = split_bf16(result)
-            split[channels * order : channels * (order + 1), lanes] = high
-            start = channels * (HALO + order)
-            split[start : start + channels, lanes] = low
+            start = channels * TERMS.index((order, 0))
+            if order == 1:
+                split[start : start + channels, lanes] = result.astype(BF16)
+            else:
+                high, low = split_bf16(result)
+                split[start : start + channels, lanes] = high
+                split[start + channels : start + 2 * channels, lanes] = low
 
 
 def stacked_weights(weights):
-    orders = weights.shape[0]
-    return jnp.concatenate(
-        [weights[k] for k in range(orders)] + [weights[k] for k in range(1, orders)], axis=1
-    )
+    return jnp.concatenate([weights[k] for k, _ in TERMS], axis=1)
 
 
 def block_list(table, homes, slots, which):
@@ -116,7 +122,7 @@
         pltpu.make_async_copy(source, target, load.at[i])
         for i, (source, target) in enumerate(
             [
-                (grad_hbm, grad),
+                *((grad_hbm.at[pl.ds(4 * i, 4)], grad.at[pl.ds(4 * i, 4)]) for i in range(channels // 4)),
                 (up_hbm, tables.at[0]),
                 (down_hbm, tables.at[1]),
                 (saved_hbm, saved),
@@ -128,14 +134,16 @@
     for copy in loads:
         copy.start()
 
-    loads[0].wait()
+    chunks = channels // 4
     for channel in range(channels):
+        if channel % 4 == 0:
+            loads[channel // 4].wait()
         flat[channel] = grad[channel].astype(F32)
     edge_first = [r for i in range(HALO) for r in (rows - 1 - i, i)]
     for r in edge_first:
         fields[0, HALO + r] = flat[:, r, :]
-    loads[1].wait()
-    loads[2].wait()
+    loads[chunks].wait()
+    loads[chunks + 1].wait()
     pl.semaphore_wait(barrier, 2)
 
     copies = []
@@ -169,7 +177,7 @@
                     field=fields.at[order, row] if order < orders - 1 else None, split=split.at[r],
                 )
 
-    for copy in loads[3:]:
+    for copy in loads[chunks + 2 :]:
         copy.wait()
     for channel in range(channels):
         flat[channel] = saved[channel].astype(F32)
@@ -200,51 +208,78 @@
         copy.wait()
 
 
-def linked_row(source, table, slots, which, target):
-    channels, columns = source.shape
+def pack_row(source, packed):
+    value = source[...]
+    half = value.shape[0] // 2
+    peak = jnp.maximum(jnp.max(jnp.abs(value), axis=1, keepdims=True), 1e-30)
+    level = jnp.round(value * (LEVELS / peak)).astype(jnp.int32)
+    packed[...] = level[:half] * 65536 + level[half:]
+    return peak * (1.0 / LEVELS)
+
+
+def unpack(total, step):
+    half = total.shape[0]
+    second = jnp.right_shift(jnp.left_shift(total, 16), 16)
+    first = jnp.right_shift(total - second, 16)
+    return first.astype(F32) * step[:half], second.astype(F32) * step[half:]
+
+
+def linked_rows(jobs, tables, slots, packed, links):
+    half, columns = packed.shape[1:]
     blocks = columns // LANES
 
-    def source_block(origin):
-        return source[:, pl.ds(pl.multiple_of(origin * LANES, LANES), LANES)]
-
-    def indices(entry, out_lanes):
-        index = jnp.broadcast_to(table[entry, :, out_lanes], (channels, LANES))
+    def source_block(which, origin):
+        return packed[which, :, pl.ds(pl.multiple_of(origin * LANES, LANES), LANES)]
+
+    def indices(which, entry, out_lanes):
+        index = jnp.broadcast_to(tables[which, entry, :, out_lanes], (half, LANES))
         return jnp.right_shift(index, 7), jnp.bitwise_and(index, LANES - 1)
 
     def moved(values, lane):
-        return jnp.take_along_axis(values, lane, axis=1, mode="promise_in_bounds")
-
+        return lax.gather(
+            values, lane[..., None], GATHER, (1, 1), mode=lax.GatherScatterMode.PROMISE_IN_BOUNDS
+        )
+
+    def put(which, out_lanes, total, step):
+        first, second = unpack(total, step)
+        links[which, 0:half, out_lanes] = first
+        links[which, half : 2 * half, out_lanes] = second
+
+    steps = {which: pack_row(source, packed.at[which]) for source, which in jobs}
     for block in range(blocks):
         out_lanes = slice(block * LANES, (block + 1) * LANES)
-        total = None
-        for entry in range(3):
-            first, second = slots[which, block, entry], slots[which, block, 3 + entry]
-            home, lane = indices(entry, out_lanes)
-            picked = jnp.where(
-                home == first,
-                moved(source_block(first), lane),
-                jnp.where(home == second, moved(source_block(second), lane), 0.0),
-            )
-            total = picked if total is None else total + picked
-        target[:, out_lanes] = total
-
-    @pl.when(slots[which, 0, 6] > 0)
-    def _():
-        @pl.loop(0, blocks)
-        def _(block):
-            out_lanes = pl.ds(pl.multiple_of(block * LANES, LANES), LANES)
-
-            def add(origin, total):
-                values = source_block(origin)
-                for entry in range(3):
-                    home, lane = indices(entry, out_lanes)
-                    total = total + jnp.where(home == origin, moved(values, lane), 0.0)
-                return total
-
-            target[:, out_lanes] = lax.fori_loop(0, blocks, add, jnp.zeros((channels, LANES), F32))
-
-
-def edge_kernel(fields, inner_split, slots, tables, split, fresh, links):
+        for _, which in jobs:
+            total = None
+            for entry in range(3):
+                first, second = slots[which, block, entry], slots[which, block, 3 + entry]
+                home, lane = indices(which, entry, out_lanes)
+                picked = jnp.where(
+                    home == first,
+                    moved(source_block(which, first), lane),
+                    jnp.where(home == second, moved(source_block(which, second), lane), 0),
+                )
+                total = picked if total is None else total + picked
+            put(which, out_lanes, total, steps[which])
+
+    for _, which in jobs:
+        @pl.when(slots[which, 0, 6] > 0)
+        def _():
+            @pl.loop(0, blocks)
+            def _(block):
+                out_lanes = pl.ds(pl.multiple_of(block * LANES, LANES), LANES)
+
+                def add(origin, total):
+                    values = source_block(which, origin)
+                    for entry in range(3):
+                        home, lane = indices(which, entry, out_lanes)
+                        total = total + jnp.where(home == origin, moved(values, lane), 0)
+                    return total
+
+                total = lax.fori_loop(0, blocks, add, jnp.zeros((half, LANES), jnp.int32))
+                put(which, out_lanes, total, steps[which])
+
+
+def edge_kernel(fields, inner_split, slots, tables, split, second, third, last_links, fresh, links, packed):
     rows = inner_split.shape[0]
     channels = fields.shape[2]
     orders = fields.shape[0] + 1
@@ -255,27 +290,35 @@
     def field(order, row):
         if order == 0 or HALO + order <= row <= bottom - order:
             return fields.at[order, row]
-        at = row - order if row <= HALO + order else HALO + row - (mirror - HALO - order + 1)
-        return fresh.at[order - 1, at]
+        side, depth = (0, row - HALO) if row <= HALO + order else (1, bottom - row)
+        if depth >= 0 and order == orders - 3:
+            return second.at[side, depth]
+        if depth >= 0 and order == orders - 2:
+            return third.at[side, depth]
+        return fresh.at[order - 1, side, depth + HALO - order]
 
     def edge(r):
         return r if r < HALO else r - rows + 2 * HALO
 
     for r in range(HALO):
+        known = slice(0, channels * TERMS.index((r + 1, 0)))
         for row in (r, rows - 1 - r):
-            known = slice(0, channels * (r + 1))
             split[edge(row), known] = inner_split[row, known]
-            if r > 0:
-                known = slice(channels * (HALO + 1), channels * (HALO + 1 + r))
-                split[edge(row), known] = inner_split[row, known]
+    for depth in range(HALO + 1):
+        for side, row in ((0, top + depth), (1, bottom - depth)):
+            if orders - 3 <= depth < HALO:
+                second[side, depth] = fields[orders - 3, row]
+            if depth >= orders - 2:
+                third[side, depth] = fields[orders - 2, row]
 
     for order in range(1, orders):
         last = order == orders - 1
-        linked_row(field(order - 1, top - 1), tables.at[0], slots, 0, links.at[0])
-        linked_row(field(order - 1, bottom + 1), tables.at[1], slots, 1, links.at[1])
-        if not last:
-            linked_row(field(order - 1, top), tables.at[2], slots, 2, links.at[2])
-            linked_row(field(order - 1, bottom), tables.at[3], slots, 3, links.at[3])
+        jobs = [(field(order - 1, top - 1), 0), (field(order - 1, bottom + 1), 1)]
+        if last:
+            linked_rows(jobs, tables, slots, packed, last_links)
+            break
+        jobs += [(field(order - 1, top), 2), (field(order - 1, bottom), 3)]
+        linked_rows(jobs, tables, slots, packed, links)
         for near in range(order, HALO + order):
             for row in (near, mirror - near):
                 upper, lower, link = field(order - 1, row - 1), field(order - 1, row + 1), None
@@ -289,19 +332,20 @@
                     upper, link = None, links.at[3]
                 sweep_row(
                     order, upper, field(order - 1, row), lower, field(order - 2, row) if order > 1 else None,
-                    link=link, field=None if last else field(order, row),
+                    link=link, field=field(order, row),
                     split=split.at[edge(row - HALO)] if top <= row <= bottom else None,
                 )
 
 
 def sum_kernel(
-    sky, inner, norm,
-    split, edge_split, acts, inner_sums, left,
-    out, weight_grad,
-    flat, part_in, part_out, in_send, in_recv, out_send, out_recv,
+    sky, inner,
+    split, edge_split, second, third, last_links, acts, inner_sums, left,
+    flat, total,
+    full, part_in, part_out, in_send, in_recv, out_send, out_recv,
 ):
-    channels, rows, columns = out.shape
-    orders = weight_grad.shape[0]
+    rows, stacked, columns = split.shape
+    known = edge_split.shape[1]
+    orders = third.shape[1]
     outer = sky // inner
     me = lax.axis_index("sky")
     slot = lax.rem(me, inner)
@@ -318,21 +362,31 @@
     for peer in peers:
         pl.semaphore_signal(barrier, inc=1, device_id={"sky": peer}, device_id_type=MESH)
 
-    def terms(r):
-        if r < HALO:
-            return edge_split[r]
-        return split[r] if r < rows - HALO else edge_split[r - rows + 2 * HALO]
+    full[:, 0:known] = edge_split[...]
+    for side in range(2):
+        def edge(depth):
+            return full.at[depth if side == 0 else 2 * HALO - 1 - depth]
+
+        sweep_row(
+            orders - 1, None, third.at[side, 0], third.at[side, 1], second.at[side, 0],
+            link=last_links.at[side], split=edge(0),
+        )
+
+        @pl.loop(1, HALO)
+        def _(depth):
+            sweep_row(
+                orders - 1, third.at[side, depth - 1], third.at[side, depth], third.at[side, depth + 1],
+                second.at[side, depth], split=edge(depth),
+            )
+
+    def edge_rows():
+        return [(r, r) for r in range(HALO)] + [(rows - 2 * HALO + r, r) for r in range(HALO, 2 * HALO)]
 
     sums = inner_sums[...]
-    for r in list(range(HALO)) + list(range(rows - HALO, rows)):
-        sums += lax.dot_general(acts[r], terms(r), CONTRACT_LAST, preferred_element_type=F32)
-    lane = lax.broadcasted_iota(jnp.int32, (channels, LANES), 1)
-    both = sums[0:channels] + sums[channels : 2 * channels]
-    first = both[:, 0:LANES]
-    second = jnp.concatenate([both[:, LANES:], jnp.zeros((channels, 2 * LANES - both.shape[1]), F32)], axis=1)
-    moved = jnp.where(lane < LANES // 2, pltpu.roll(first, LANES // 2, 1), pltpu.roll(second, LANES // 2, 1))
-    wide = channels * orders
-    part_in[slot] = jnp.where(lane < wide, first, 0.0) + jnp.where((lane >= channels) & (lane < wide), moved, 0.0)
+    for r, at in edge_rows():
+        sums += lax.dot_general(acts[r], full[at], CONTRACT_LAST, preferred_element_type=F32)
+    channels = sums.shape[0] // 2
+    part_in[slot] = sums[0:channels] + sums[channels : 2 * channels]
     pl.semaphore_wait(barrier, len(peers))
 
     def exchange(buffer, own, count, peer_of, send, recv):
@@ -350,15 +404,23 @@
         return functools.reduce(lambda total, i: total + buffer[i], range(1, len(copies) + 1), buffer[0])
 
     copies = exchange(part_in, slot, inner, in_peer, in_send, in_recv)
-    for r in range(rows):
-        flat[:, r, :] = jnp.dot(left[...], terms(r), preferred_element_type=F32)
+    for r, at in edge_rows():
+        flat[:, r, :] = jnp.dot(left[...], full[at], preferred_element_type=F32)
     part_out[group] = total_of(part_in, copies)
     copies = exchange(part_out, group, outer, out_peer, out_send, out_recv)
+    for r in range(HALO, rows - HALO):
+        flat[:, r, :] = jnp.dot(left[...], split[r], preferred_element_type=F32)
+    total[...] = total_of(part_out, copies)
+
+
+def result_kernel(norm, flat, total, out, weight_grad):
+    channels = out.shape[0]
     for channel in range(channels):
         out[channel] = flat[channel].astype(BF16)
-    total = total_of(part_out, copies) * norm
-    for k in range(orders):
-        weight_grad[k] = total[:, channels * k : channels * (k + 1)]
+    scaled = total[...] * norm
+    for k in range(weight_grad.shape[0]):
+        parts = [scaled[:, channels * i : channels * (i + 1)] for i, (order, _) in enumerate(TERMS) if order == k]
+        weight_grad[k] = functools.reduce(jnp.add, parts)
 
 
 def on_device(sky, saved_acts, scales, grad_out, weights, edge_up, edge_down):
@@ -368,7 +430,9 @@
     inner = min(8, sky)
     outer = sky // inner
     norm = 1.0 / math.sqrt(rows * columns * sky)
-    stacked = channels * (2 * orders - 1)
+    stacked = channels * len(TERMS)
+    known = channels * TERMS.index((orders - 1, 0))
+    edge = 2 * HALO
     vmem = pl.BlockSpec(memory_space=pltpu.VMEM)
     smem = pl.BlockSpec(memory_space=pltpu.SMEM)
     hbm = pl.BlockSpec(memory_space=pltpu.HBM)
@@ -397,41 +461,55 @@
             pltpu.VMEM((rows, channels, columns), F32),
             pltpu.VMEM((rows, channels, blocks), F32),
             pltpu.VMEM((3, columns // LANES, LANES), jnp.int32),
-            dma((2, HALO)), dma((2, HALO)), dma((2,)), dma((2,)), dma((6,)),
+            dma((2, HALO)), dma((2, HALO)), dma((2,)), dma((2,)), dma((channels // 4 + 5,)),
         ],
         compiler_params=pltpu.CompilerParams(
             collective_id=0, has_side_effects=True, vmem_limit_bytes=12 * 2**20
         ),
         name="exchange",
     )(*(pltpu.with_memory_space_constraint(x, pltpu.HBM) for x in (saved_acts, scales, grad_out, weights, up, down)))
-    edge_split = pl.pallas_call(
+    edge_split, second, third, last_links = pl.pallas_call(
         edge_kernel,
-        out_shape=shape((2 * HALO, stacked, columns), BF16),
+        out_shape=(
+            shape((edge, known, columns), BF16),
+            shape((2, HALO, channels, columns), F32),
+            shape((2, HALO + 1, channels, columns), F32),
+            shape((2, channels, columns), F32),
+        ),
         in_specs=[vmem, vmem, smem, vmem],
-        out_specs=vmem,
+        out_specs=(vmem,) * 4,
         scratch_shapes=[
-            pltpu.VMEM((orders - 2, 2 * HALO, channels, columns), F32),
+            pltpu.VMEM((orders - 2, 2, HALO + 1, channels, columns), F32),
             pltpu.VMEM((4, channels, columns), F32),
+            pltpu.VMEM((4, channels // 2, columns), jnp.int32),
         ],
         compiler_params=pltpu.CompilerParams(vmem_limit_bytes=12 * 2**20),
         name="edges",
     )(fields, split, slots, tables)
-    return pl.pallas_call(
-        functools.partial(sum_kernel, sky, inner, norm),
-        out_shape=(shape((channels, rows, columns), BF16), shape((orders, channels, channels), F32)),
-        in_specs=[vmem] * 5,
+    flat, total = pl.pallas_call(
+        functools.partial(sum_kernel, sky, inner),
+        out_shape=(shape((channels, rows, columns), F32), shape((channels, stacked), F32)),
+        in_specs=[vmem] * 8,
         out_specs=(vmem, vmem),
         scratch_shapes=[
-            pltpu.VMEM((channels, rows, columns), F32),
-            pltpu.VMEM((inner, channels, LANES), F32),
-            pltpu.VMEM((outer, channels, LANES), F32),
+            pltpu.VMEM((edge, stacked, columns), BF16),
+            pltpu.VMEM((inner, channels, stacked), F32),
+            pltpu.VMEM((outer, channels, stacked), F32),
             dma((inner,)), dma((inner,)), dma((outer,)), dma((outer,)),
         ],
         compiler_params=pltpu.CompilerParams(
             collective_id=1, has_side_effects=True, vmem_limit_bytes=12 * 2**20
         ),
         name="sky_sum",
-    )(split, edge_split, acts, sums, left)
+    )(split, edge_split, second, third, last_links, acts, sums, left)
+    return pl.pallas_call(
+        functools.partial(result_kernel, norm),
+        out_shape=(shape((channels, rows, columns), BF16), shape((orders, channels, channels), F32)),
+        in_specs=[vmem] * 2,
+        out_specs=(vmem, vmem),
+        compiler_params=pltpu.CompilerParams(vmem_limit_bytes=12 * 2**20),
+        name="results",
+    )(flat, total)
 
 
 def solution(mesh):

time: 42.3 us -> 40.1 us (0.948)
  local copies, waits for them, and re-layouts: 1.59 us -> 0 us
  Pallas kernels: 39.7 us -> 39.2 us
    unnamed x2 -> x0, local copies, waits for them, and re-layouts: 1.59 us -> none
    pallas_call x2 -> x3, Pallas kernels: 21.2 us -> 20.9 us  [the longest x1 12.3 us: on_device(): pl.pallas_call(functools.partial(sum_kernel, sky, inner), out_shape=(shap...]
where the time goes in v3:
time: 40.1 us; the launch traced here: 39.8 us
  Pallas kernels  39.2 us (98%)
  between operations  0.66 us (2%)
    pallas_call x1, Pallas kernels, on_device(): pl.pallas_call(functools.partial(exchange_kernel, sky), out_shape=(shape(...  18.3 us
    pallas_call x1, Pallas kernels, on_device(): pl.pallas_call(functools.partial(sum_kernel, sky, inner), out_shape=(shap...  12.3 us
    pallas_call x1, Pallas kernels, on_device(): pl.pallas_call(edge_kernel, out_shape=(shape((edge, known, columns), BF16...  7.47 us
    pallas_call x1, Pallas kernels, on_device(): pl.pallas_call(functools.partial(result_kernel, norm), out_shape=(shape((...  1.13 us

profile of v3, /device:TPU:4, one launch (start us, length us, event | category | flops | bytes accessed | tf_op | source)
XLA Modules:
  0.0 39.8 jit_solution(16809253551024773477)
XLA Ops:
  0.6 18.3 %exchange.1 = (f32[4,24,16,2048]{3,2,1,0:T(8,128)S(1)}, bf16[16,128,2048]{2,1,0:T(8,128)(2,1)S(1)}, bf16[16,32,2048]{2,1,0:T(8,128)(2,1)S(1)}, f32[32,128]{1,0:T...) custom-call(bf16[16,16,2048]{2,1,0:T(8,128)(2,1)} %saved_hbm.1, ...), custom_call_target="tpu_custom_call" | custom-call | tf_op jit(solution)/shard_map/exchange/pallas_call | solution.py:442
  19.0 7.5 %edges.1 = (bf16[8,96,2048]{2,1,0:T(8,128)(2,1)S(1)}, f32[2,4,16,2048]{3,2,1,0:T(8,128)S(1)}, f32[2,5,16,2048]{3,2,1,0:T(8,128)S(1)}, f32[2,16,2048]{2,1,0:T(8,128)S(1)}) custom-call(f32[4,24,16,2048]{3,2,1,0:T(8,128)S(1)} %get-tuple-element.16.fields, bf16[16,128,2048]{2,1,0:T(8,128)(2,1)S(1)} %get-tuple-element.15.inner_split.split, ...), custom_call_target="tpu_custom_call" | custom-call | tf_op jit(solution)/shard_map/edges/pallas_call | solution.py:471
  26.4 12.3 %sky_sum.1 = (f32[16,16,2048]{2,1,0:T(8,128)S(1)}, f32[16,128]{1,0:T(8,128)S(1)}) custom-call(bf16[16,128,2048]{2,1,0:T(8,128)(2,1)S(1)} %get-tuple-element.15.inner_split.split, bf16[8,96,2048]{2,1,0:T(8,128)(2,1)S(1)} %get-tuple-element.19.edge_split, f32[2,4,16,2048]{3,2,1,0:T(8,128)S(1)} %get-tuple-element.20.second, ...), custom_call_target="tpu_custom_call" | custom-call | tf_op jit(solution)/shard_map/sky_sum/pallas_call | solution.py:489
  38.7 1.1 %results.1 = (bf16[16,16,2048]{2,1,0:T(8,128)(2,1)}, f32[5,16,16]{2,1,0:T(8,128)}) custom-call(f32[16,16,2048]{2,1,0:T(8,128)S(1)} %get-tuple-element.26.flat, f32[16,128]{1,0:T(8,128)S(1)} %get-tuple-element.27.total), custom_call_target="tpu_custom_call" | custom-call | tf_op jit(solution)/shard_map/results/pallas_call | solution.py:505

commit v4 on v3

--- a/solution.py
+++ b/solution.py
@@ -79,23 +79,26 @@
     return jnp.concatenate([weights[k] for k, _ in TERMS], axis=1)
 
 
-def block_list(table, homes, slots, which):
+def block_list(table, arranged, codes, slots, which):
     blocks = table.shape[-1] // LANES
     for entry in range(3):
         for block in range(blocks):
-            homes[entry, block : block + 1, :] = jnp.right_shift(
-                table[entry, :, block * LANES : (block + 1) * LANES], 7
-            )
+            arranged[entry, block : block + 1, :] = table[entry, :, block * LANES : (block + 1) * LANES]
     lane = lax.broadcasted_iota(jnp.int32, (blocks, LANES), 1)
     packed = jnp.zeros((blocks, LANES), jnp.int32)
     more = jnp.zeros((blocks, 1), jnp.int32)
     for entry in range(3):
-        home = homes[entry]
+        index = arranged[entry]
+        home = jnp.right_shift(index, 7)
         first = jnp.min(home, axis=1, keepdims=True)
         second = jnp.min(jnp.where(home > first, home, blocks), axis=1, keepdims=True)
         third = jnp.min(jnp.where(home > second, home, blocks), axis=1, keepdims=True)
-        packed = jnp.where(lane == entry, jnp.minimum(first, blocks - 1), packed)
-        packed = jnp.where(lane == 3 + entry, jnp.minimum(second, blocks - 1), packed)
+        first = jnp.minimum(first, blocks - 1)
+        second = jnp.minimum(second, blocks - 1)
+        slot = jnp.where(home == first, 0, jnp.where(home == second, LANES, 2 * LANES))
+        codes[which, entry] = jnp.bitwise_and(index, LANES - 1) + slot
+        packed = jnp.where(lane == entry, first, packed)
+        packed = jnp.where(lane == 3 + entry, second, packed)
         more = jnp.maximum(more, (third < blocks).astype(jnp.int32))
     slots[which] = jnp.where(lane == 6, jnp.max(more, axis=0, keepdims=True), packed)
 
@@ -103,8 +106,8 @@
 def exchange_kernel(
     sky,
     saved_hbm, scales_hbm, grad_hbm, weights_hbm, up_hbm, down_hbm,
-    fields, split, acts, sums, slots, tables, left,
-    saved, scales, grad, weights, flat, rows_x, scale_rows, homes,
+    fields, split, acts, slots, codes, tables, left,
+    saved, scales, grad, weights, flat, rows_x, scale_rows, arranged,
     halo_send, halo_recv, table_send, table_recv, load,
 ):
     channels, rows, columns = saved.shape
@@ -146,16 +149,15 @@
     loads[chunks + 1].wait()
     pl.semaphore_wait(barrier, 2)
 
-    copies = []
+    copies = [
+        remote(tables.at[0], tables.at[3], table_send.at[0], table_recv.at[0], before),
+        remote(tables.at[1], tables.at[2], table_send.at[1], table_recv.at[1], after),
+    ]
     for i in range(HALO):
         copies += [
             remote(fields.at[0, HALO + i], fields.at[0, HALO + rows + i], halo_send.at[0, i], halo_recv.at[0, i], before),
             remote(fields.at[0, HALO + rows - 1 - i], fields.at[0, HALO - 1 - i], halo_send.at[1, i], halo_recv.at[1, i], after),
         ]
-    copies += [
-        remote(tables.at[0], tables.at[3], table_send.at[0], table_recv.at[0], before),
-        remote(tables.at[1], tables.at[2], table_send.at[1], table_recv.at[1], after),
-    ]
     for copy in copies:
         copy.start()
 
@@ -194,17 +196,13 @@
             acts[r, channels : 2 * channels, lanes] = low
 
     left[...] = stacked_weights(weights)
-    sums[...] = jnp.zeros_like(sums)
-    for r in range(HALO, rows - HALO):
-        sums[...] += lax.dot_general(acts[r], split[r], CONTRACT_LAST, preferred_element_type=F32)
-
-    block_list(tables.at[0], homes, slots, 0)
-    block_list(tables.at[1], homes, slots, 1)
-    for copy in copies[2 * HALO :]:
+    block_list(tables.at[0], arranged, codes, slots, 0)
+    block_list(tables.at[1], arranged, codes, slots, 1)
+    for copy in copies[:2]:
         copy.wait()
-    block_list(tables.at[2], homes, slots, 2)
-    block_list(tables.at[3], homes, slots, 3)
-    for copy in copies[: 2 * HALO]:
+    block_list(tables.at[2], arranged, codes, slots, 2)
+    block_list(tables.at[3], arranged, codes, slots, 3)
+    for copy in copies[2:]:
         copy.wait()
 
 
@@ -213,7 +211,9 @@
     half = value.shape[0] // 2
     peak = jnp.maximum(jnp.max(jnp.abs(value), axis=1, keepdims=True), 1e-30)
     level = jnp.round(value * (LEVELS / peak)).astype(jnp.int32)
-    packed[...] = level[:half] * 65536 + level[half:]
+    both = level[:half] * 65536 + level[half:]
+    for block in range(packed.shape[0]):
+        packed[block] = both[:, block * LANES : (block + 1) * LANES]
     return peak * (1.0 / LEVELS)
 
 
@@ -224,16 +224,8 @@
     return first.astype(F32) * step[:half], second.astype(F32) * step[half:]
 
 
-def linked_rows(jobs, tables, slots, packed, links):
-    half, columns = packed.shape[1:]
-    blocks = columns // LANES
-
-    def source_block(which, origin):
-        return packed[which, :, pl.ds(pl.multiple_of(origin * LANES, LANES), LANES)]
-
-    def indices(which, entry, out_lanes):
-        index = jnp.broadcast_to(tables[which, entry, :, out_lanes], (half, LANES))
-        return jnp.right_shift(index, 7), jnp.bitwise_and(index, LANES - 1)
+def linked_rows(jobs, tables, codes, slots, packed, links):
+    blocks, half = packed.shape[1:3]
 
     def moved(values, lane):
         return lax.gather(
@@ -252,11 +244,12 @@
             total = None
             for entry in range(3):
                 first, second = slots[which, block, entry], slots[which, block, 3 + entry]
-                home, lane = indices(which, entry, out_lanes)
+                code = jnp.broadcast_to(codes[which, entry, block : block + 1, :], (half, LANES))
+                lane = jnp.bitwise_and(code, LANES - 1)
                 picked = jnp.where(
-                    home == first,
-                    moved(source_block(which, first), lane),
-                    jnp.where(home == second, moved(source_block(which, second), lane), 0),
+                    code < LANES,
+                    moved(packed[which, first], lane),
+                    jnp.where(code < 2 * LANES, moved(packed[which, second], lane), 0),
                 )
                 total = picked if total is None else total + picked
             put(which, out_lanes, total, steps[which])
@@ -269,18 +262,18 @@
                 out_lanes = pl.ds(pl.multiple_of(block * LANES, LANES), LANES)
 
                 def add(origin, total):
-                    values = source_block(which, origin)
+                    values = packed[which, origin]
                     for entry in range(3):
-                        home, lane = indices(which, entry, out_lanes)
-                        total = total + jnp.where(home == origin, moved(values, lane), 0)
+                        index = jnp.broadcast_to(tables[which, entry, :, out_lanes], (half, LANES))
+                        arrived = moved(values, jnp.bitwise_and(index, LANES - 1))
+                        total = total + jnp.where(jnp.right_shift(index, 7) == origin, arrived, 0)
                     return total
 
                 total = lax.fori_loop(0, blocks, add, jnp.zeros((half, LANES), jnp.int32))
                 put(which, out_lanes, total, steps[which])
 
 
-def edge_kernel(fields, inner_split, slots, tables, split, second, third, last_links, fresh, links, packed):
-    rows = inner_split.shape[0]
+def edge_kernel(rows, fields, slots, codes, tables, split, second, third, last_links, fresh, links, packed):
     channels = fields.shape[2]
     orders = fields.shape[0] + 1
     top = HALO
@@ -300,25 +293,14 @@
     def edge(r):
         return r if r < HALO else r - rows + 2 * HALO
 
-    for r in range(HALO):
-        known = slice(0, channels * TERMS.index((r + 1, 0)))
-        for row in (r, rows - 1 - r):
-            split[edge(row), known] = inner_split[row, known]
-    for depth in range(HALO + 1):
-        for side, row in ((0, top + depth), (1, bottom - depth)):
-            if orders - 3 <= depth < HALO:
-                second[side, depth] = fields[orders - 3, row]
-            if depth >= orders - 2:
-                third[side, depth] = fields[orders - 2, row]
-
     for order in range(1, orders):
         last = order == orders - 1
         jobs = [(field(order - 1, top - 1), 0), (field(order - 1, bottom + 1), 1)]
         if last:
-            linked_rows(jobs, tables, slots, packed, last_links)
+            linked_rows(jobs, tables, codes, slots, packed, last_links)
             break
         jobs += [(field(order - 1, top), 2), (field(order - 1, bottom), 3)]
-        linked_rows(jobs, tables, slots, packed, links)
+        linked_rows(jobs, tables, codes, slots, packed, links)
         for near in range(order, HALO + order):
             for row in (near, mirror - near):
                 upper, lower, link = field(order - 1, row - 1), field(order - 1, row + 1), None
@@ -339,13 +321,13 @@
 
 def sum_kernel(
     sky, inner,
-    split, edge_split, second, third, last_links, acts, inner_sums, left,
+    fields, split, edge_split, fresh_second, fresh_third, last_links, acts, left,
     flat, total,
-    full, part_in, part_out, in_send, in_recv, out_send, out_recv,
+    full, second, third, part_in, part_out, in_send, in_recv, out_send, out_recv,
 ):
     rows, stacked, columns = split.shape
-    known = edge_split.shape[1]
-    orders = third.shape[1]
+    orders = HALO + 1
+    channels = stacked // len(TERMS)
     outer = sky // inner
     me = lax.axis_index("sky")
     slot = lax.rem(me, inner)
@@ -362,7 +344,21 @@
     for peer in peers:
         pl.semaphore_signal(barrier, inc=1, device_id={"sky": peer}, device_id_type=MESH)
 
-    full[:, 0:known] = edge_split[...]
+    for depth in range(HALO + 1):
+        first = channels * TERMS.index((min(depth + 1, orders - 1), 0))
+        known = channels * TERMS.index((orders - 1, 0))
+        for side in range(2):
+            row = depth if side == 0 else rows - 1 - depth
+            if depth < HALO:
+                at = depth if side == 0 else 2 * HALO - 1 - depth
+                full[at, 0:first] = split[row, 0:first]
+                if first < known:
+                    full[at, first:known] = edge_split[at, first:known]
+                old = depth >= orders - 3
+                second[side, depth] = fields[orders - 3, HALO + row] if old else fresh_second[side, depth]
+            old = depth >= orders - 2
+            third[side, depth] = fields[orders - 2, HALO + row] if old else fresh_third[side, depth]
+
     for side in range(2):
         def edge(depth):
             return full.at[depth if side == 0 else 2 * HALO - 1 - depth]
@@ -382,10 +378,11 @@
     def edge_rows():
         return [(r, r) for r in range(HALO)] + [(rows - 2 * HALO + r, r) for r in range(HALO, 2 * HALO)]
 
-    sums = inner_sums[...]
+    sums = jnp.zeros((acts.shape[1], stacked), F32)
+    for r in range(HALO, rows - HALO):
+        sums += lax.dot_general(acts[r], split[r], CONTRACT_LAST, preferred_element_type=F32)
     for r, at in edge_rows():
         sums += lax.dot_general(acts[r], full[at], CONTRACT_LAST, preferred_element_type=F32)
-    channels = sums.shape[0] // 2
     part_in[slot] = sums[0:channels] + sums[channels : 2 * channels]
     pl.semaphore_wait(barrier, len(peers))
 
@@ -413,14 +410,21 @@
     total[...] = total_of(part_out, copies)
 
 
-def result_kernel(norm, flat, total, out, weight_grad):
-    channels = out.shape[0]
-    for channel in range(channels):
-        out[channel] = flat[channel].astype(BF16)
+def result_kernel(norm, flat, total, out, weight_grad, rounded, store):
+    channels = flat.shape[0]
+    copies = []
+    for start in range(0, channels, 4):
+        for channel in range(start, start + 4):
+            rounded[channel] = flat[channel].astype(BF16)
+        part = pl.ds(start, 4)
+        copies.append(pltpu.make_async_copy(rounded.at[part], out.at[part], store.at[start // 4]))
+        copies[-1].start()
     scaled = total[...] * norm
     for k in range(weight_grad.shape[0]):
         parts = [scaled[:, channels * i : channels * (i + 1)] for i, (order, _) in enumerate(TERMS) if order == k]
         weight_grad[k] = functools.reduce(jnp.add, parts)
+    for copy in copies:
+        copy.wait()
 
 
 def on_device(sky, saved_acts, scales, grad_out, weights, edge_up, edge_down):
@@ -439,14 +443,14 @@
     dma = pltpu.SemaphoreType.DMA
     shape = jax.ShapeDtypeStruct
     up, down = jnp.transpose(edge_up, (1, 0, 2)), jnp.transpose(edge_down, (1, 0, 2))
-    fields, split, acts, sums, slots, tables, left = pl.pallas_call(
+    fields, split, acts, slots, codes, tables, left = pl.pallas_call(
         functools.partial(exchange_kernel, sky),
         out_shape=(
             shape((orders - 1, rows + 2 * HALO, channels, columns), F32),
             shape((rows, stacked, columns), BF16),
             shape((rows, 2 * channels, columns), BF16),
-            shape((2 * channels, stacked), F32),
             shape((4, columns // LANES, LANES), jnp.int32),
+            shape((4, 3, columns // LANES, LANES), jnp.int32),
             shape((4, 3, 1, columns), jnp.int32),
             shape((channels, stacked), BF16),
         ),
@@ -469,23 +473,23 @@
         name="exchange",
     )(*(pltpu.with_memory_space_constraint(x, pltpu.HBM) for x in (saved_acts, scales, grad_out, weights, up, down)))
     edge_split, second, third, last_links = pl.pallas_call(
-        edge_kernel,
+        functools.partial(edge_kernel, rows),
         out_shape=(
             shape((edge, known, columns), BF16),
-            shape((2, HALO, channels, columns), F32),
-            shape((2, HALO + 1, channels, columns), F32),
+            shape((2, HALO - 2, channels, columns), F32),
+            shape((2, HALO - 1, channels, columns), F32),
             shape((2, channels, columns), F32),
         ),
-        in_specs=[vmem, vmem, smem, vmem],
+        in_specs=[vmem, smem, vmem, vmem],
         out_specs=(vmem,) * 4,
         scratch_shapes=[
             pltpu.VMEM((orders - 2, 2, HALO + 1, channels, columns), F32),
             pltpu.VMEM((4, channels, columns), F32),
-            pltpu.VMEM((4, channels // 2, columns), jnp.int32),
+            pltpu.VMEM((4, columns // LANES, channels // 2, LANES), jnp.int32),
         ],
         compiler_params=pltpu.CompilerParams(vmem_limit_bytes=12 * 2**20),
         name="edges",
-    )(fields, split, slots, tables)
+    )(fields, slots, codes, tables)
     flat, total = pl.pallas_call(
         functools.partial(sum_kernel, sky, inner),
         out_shape=(shape((channels, rows, columns), F32), shape((channels, stacked), F32)),
@@ -493,6 +497,8 @@
         out_specs=(vmem, vmem),
         scratch_shapes=[
             pltpu.VMEM((edge, stacked, columns), BF16),
+            pltpu.VMEM((2, HALO, channels, columns), F32),
+            pltpu.VMEM((2, HALO + 1, channels, columns), F32),
             pltpu.VMEM((inner, channels, stacked), F32),
             pltpu.VMEM((outer, channels, stacked), F32),
             dma((inner,)), dma((inner,)), dma((outer,)), dma((outer,)),
@@ -501,12 +507,13 @@
             collective_id=1, has_side_effects=True, vmem_limit_bytes=12 * 2**20
         ),
         name="sky_sum",
-    )(split, edge_split, second, third, last_links, acts, sums, left)
+    )(fields, split, edge_split, second, third, last_links, acts, left)
     return pl.pallas_call(
         functools.partial(result_kernel, norm),
         out_shape=(shape((channels, rows, columns), BF16), shape((orders, channels, channels), F32)),
         in_specs=[vmem] * 2,
-        out_specs=(vmem, vmem),
+        out_specs=(hbm, vmem),
+        scratch_shapes=[pltpu.VMEM((channels, rows, columns), BF16), dma((channels // 4,))],
         compiler_params=pltpu.CompilerParams(vmem_limit_bytes=12 * 2**20),
         name="results",
     )(flat, total)

time: 40.1 us -> 41.8 us (1.042)
  Pallas kernels: 39.2 us -> 40.3 us
    pallas_call x1, Pallas kernels: 12.3 us -> 13.8 us  [on_device(): pl.pallas_call(functools.partial(sum_kernel, sky, inner), out_shape=(shap...]
    pallas_call x1, Pallas kernels: 18.3 us -> 17.4 us  [on_device(): pl.pallas_call(functools.partial(exchange_kernel, sky), out_shape=(shape(...]
    pallas_call x1, Pallas kernels: 1.13 us -> 1.69 us  [on_device(): pl.pallas_call(functools.partial(result_kernel, norm), out_shape=(shape((...]
where the time goes in v4:
time: 41.8 us; the launch traced here: 41.2 us
  Pallas kernels  40.3 us (96%)
  between operations  0.82 us (2%)
    pallas_call x1, Pallas kernels, on_device(): pl.pallas_call(functools.partial(exchange_kernel, sky), out_shape=(shape(...  17.4 us
    pallas_call x1, Pallas kernels, on_device(): pl.pallas_call(functools.partial(sum_kernel, sky, inner), out_shape=(shap...  13.8 us
    pallas_call x1, Pallas kernels, on_device(): pl.pallas_call(functools.partial(edge_kernel, rows), out_shape=(shape((ed...  7.4 us
    pallas_call x1, Pallas kernels, on_device(): pl.pallas_call(functools.partial(result_kernel, norm), out_shape=(shape((...  1.69 us

profile of v4, /device:TPU:4, one launch (start us, length us, event | category | flops | bytes accessed | tf_op | source)
XLA Modules:
  0.0 41.2 jit_solution(3398304254681440476)
XLA Ops:
  0.6 17.4 %exchange.1 = (f32[4,24,16,2048]{3,2,1,0:T(8,128)S(1)}, bf16[16,128,2048]{2,1,0:T(8,128)(2,1)S(1)}, bf16[16,32,2048]{2,1,0:T(8,128)(2,1)S(1)}, s32[4,16,128]{2,1...) custom-call(bf16[16,16,2048]{2,1,0:T(8,128)(2,1)} %saved_hbm.1, ...), custom_call_target="tpu_custom_call" | custom-call | tf_op jit(solution)/shard_map/exchange/pallas_call | solution.py:446
  18.1 7.4 %edges.1 = (bf16[8,96,2048]{2,1,0:T(8,128)(2,1)S(1)}, f32[2,2,16,2048]{3,2,1,0:T(8,128)S(1)}, f32[2,3,16,2048]{3,2,1,0:T(8,128)S(1)}, f32[2,16,2048]{2,1,0:T(8,128)S(1)}) custom-call(f32[4,24,16,2048]{3,2,1,0:T(8,128)S(1)} %get-tuple-element.15.fields, s32[4,16,128]{2,1,0:T(8,128)S(1)} %get-tuple-element.17.slots, ...), custom_call_target="tpu_custom_call" | custom-call | tf_op jit(solution)/shard_map/edges/pallas_call | solution.py:475
  25.5 13.8 %sky_sum.1 = (f32[16,16,2048]{2,1,0:T(8,128)S(1)}, f32[16,128]{1,0:T(8,128)S(1)}) custom-call(f32[4,24,16,2048]{3,2,1,0:T(8,128)S(1)} %get-tuple-element.15.fields, bf16[16,128,2048]{2,1,0:T(8,128)(2,1)S(1)} %get-tuple-element.16.split, bf16[8,96,2048]{2,1,0:T(8,128)(2,1)S(1)} %get-tuple-element.20.edge_split, ...), custom_call_target="tpu_custom_call" | custom-call | tf_op jit(solution)/shard_map/sky_sum/pallas_call | solution.py:493
  39.3 1.7 %results.1 = (bf16[16,16,2048]{2,1,0:T(8,128)(2,1)}, f32[5,16,16]{2,1,0:T(8,128)}) custom-call(f32[16,16,2048]{2,1,0:T(8,128)S(1)} %get-tuple-element.26.flat, f32[16,128]{1,0:T(8,128)S(1)} %get-tuple-element.27.total), custom_call_target="tpu_custom_call" | custom-call | tf_op jit(solution)/shard_map/results/pallas_call | solution.py:511

commit v5 on v4

--- a/solution.py
+++ b/solution.py
@@ -35,9 +35,11 @@
     )
 
 
-def sweep_row(order, upper, middle, lower, older, link=None, field=None, split=None):
+def sweep_row(order, upper, middle, lower, older, link=None, field=None, split=None, start=None):
     channels, columns = middle.shape
     blocks = columns // LANES
+    if start is None:
+        start = channels * TERMS.index((order, 0))
     lane = lax.broadcasted_iota(jnp.int32, (channels, LANES), 1)
     sums = []
     for block in range(blocks):
@@ -66,7 +68,6 @@
         if field is not None:
             field[:, lanes] = result
         if split is not None:
-            start = channels * TERMS.index((order, 0))
             if order == 1:
                 split[start : start + channels, lanes] = result.astype(BF16)
             else:
@@ -106,7 +107,7 @@
 def exchange_kernel(
     sky,
     saved_hbm, scales_hbm, grad_hbm, weights_hbm, up_hbm, down_hbm,
-    fields, split, acts, slots, codes, tables, left,
+    fields, split, acts, sums, slots, codes, tables, left,
     saved, scales, grad, weights, flat, rows_x, scale_rows, arranged,
     halo_send, halo_recv, table_send, table_recv, load,
 ):
@@ -196,6 +197,10 @@
             acts[r, channels : 2 * channels, lanes] = low
 
     left[...] = stacked_weights(weights)
+    total = jnp.zeros(sums.shape, F32)
+    for r in range(HALO, rows - HALO):
+        total += lax.dot_general(acts[r], split[r], CONTRACT_LAST, preferred_element_type=F32)
+    sums[...] = total
     block_list(tables.at[0], arranged, codes, slots, 0)
     block_list(tables.at[1], arranged, codes, slots, 1)
     for copy in copies[:2]:
@@ -224,7 +229,7 @@
     return first.astype(F32) * step[:half], second.astype(F32) * step[half:]
 
 
-def linked_rows(jobs, tables, codes, slots, packed, links):
+def linked_rows(jobs, tables, codes, slots, packed, links, between=()):
     blocks, half = packed.shape[1:3]
 
     def moved(values, lane):
@@ -244,17 +249,17 @@
             total = None
             for entry in range(3):
                 first, second = slots[which, block, entry], slots[which, block, 3 + entry]
-                code = jnp.broadcast_to(codes[which, entry, block : block + 1, :], (half, LANES))
-                lane = jnp.bitwise_and(code, LANES - 1)
-                picked = jnp.where(
-                    code < LANES,
-                    moved(packed[which, first], lane),
-                    jnp.where(code < 2 * LANES, moved(packed[which, second], lane), 0),
-                )
+                code = jnp.broadcast_to(codes[which, entry, block : block + 1, :], (2 * half, LANES))
+                values = jnp.concatenate([packed[which, first], packed[which, second]], axis=0)
+                arrived = moved(values, jnp.bitwise_and(code, LANES - 1))
+                code = code[:half]
+                picked = jnp.where(code < LANES, arrived[:half], jnp.where(code < 2 * LANES, arrived[half:], 0))
                 total = picked if total is None else total + picked
             put(which, out_lanes, total, steps[which])
-
-    for _, which in jobs:
+        for work in between[block::blocks]:
+            work()
+
+    def general(which):
         @pl.when(slots[which, 0, 6] > 0)
         def _():
             @pl.loop(0, blocks)
@@ -272,8 +277,14 @@
                 total = lax.fori_loop(0, blocks, add, jnp.zeros((half, LANES), jnp.int32))
                 put(which, out_lanes, total, steps[which])
 
-
-def edge_kernel(rows, fields, slots, codes, tables, split, second, third, last_links, fresh, links, packed):
+    @pl.when(functools.reduce(jnp.maximum, [slots[which, 0, 6] for _, which in jobs]) > 0)
+    def _():
+        for _, which in jobs:
+            general(which)
+
+
+def edge_kernel(fields, inner_split, slots, codes, tables, split, second, third, last_links, fresh, links, packed):
+    rows = inner_split.shape[0]
     channels = fields.shape[2]
     orders = fields.shape[0] + 1
     top = HALO
@@ -293,37 +304,62 @@
     def edge(r):
         return r if r < HALO else r - rows + 2 * HALO
 
+    def copy_terms(row, depth):
+        known = slice(0, channels * TERMS.index((depth + 1, 0)))
+        split[edge(row), known] = inner_split[row, known]
+
+    def copy_field(target, order, side, depth):
+        target[side, depth] = fields[order, top + depth if side == 0 else bottom - depth]
+
+    copies = []
+    for depth in range(HALO + 1):
+        for side in range(2):
+            row = depth if side == 0 else rows - 1 - depth
+            if depth < HALO:
+                copies.append(functools.partial(copy_terms, row, depth))
+            if orders - 3 <= depth < HALO:
+                copies.append(functools.partial(copy_field, second, orders - 3, side, depth))
+            if depth >= orders - 2:
+                copies.append(functools.partial(copy_field, third, orders - 2, side, depth))
+
+    def sweep(order, row):
+        last = order == orders - 1
+        upper, lower, link = field(order - 1, row - 1), field(order - 1, row + 1), None
+        if row == top:
+            upper, link = None, links.at[0]
+        elif row == bottom:
+            lower, link = None, links.at[1]
+        elif row == top - 1:
+            lower, link = None, links.at[2]
+        elif row == bottom + 1:
+            upper, link = None, links.at[3]
+        sweep_row(
+            order, upper, field(order - 1, row), lower, field(order - 2, row) if order > 1 else None,
+            link=link, field=None if last else field(order, row),
+            split=split.at[edge(row - HALO)] if top <= row <= bottom else None,
+        )
+
     for order in range(1, orders):
         last = order == orders - 1
         jobs = [(field(order - 1, top - 1), 0), (field(order - 1, bottom + 1), 1)]
-        if last:
-            linked_rows(jobs, tables, codes, slots, packed, last_links)
-            break
-        jobs += [(field(order - 1, top), 2), (field(order - 1, bottom), 3)]
-        linked_rows(jobs, tables, codes, slots, packed, links)
-        for near in range(order, HALO + order):
-            for row in (near, mirror - near):
-                upper, lower, link = field(order - 1, row - 1), field(order - 1, row + 1), None
-                if row == top:
-                    upper, link = None, links.at[0]
-                elif row == bottom:
-                    lower, link = None, links.at[1]
-                elif row == top - 1:
-                    lower, link = None, links.at[2]
-                elif row == bottom + 1:
-                    upper, link = None, links.at[3]
-                sweep_row(
-                    order, upper, field(order - 1, row), lower, field(order - 2, row) if order > 1 else None,
-                    link=link, field=field(order, row),
-                    split=split.at[edge(row - HALO)] if top <= row <= bottom else None,
-                )
+        if not last:
+            jobs += [(field(order - 1, top), 2), (field(order - 1, bottom), 3)]
+        swept = [row for near in range(order, HALO + order) for row in (near, mirror - near)]
+        linked = [row for row in swept if row in (top - 1, top, bottom, bottom + 1)]
+        between = [functools.partial(sweep, order, row) for row in swept if row not in linked]
+        if order == 1:
+            between += copies
+        linked_rows(jobs, tables, codes, slots, packed, last_links if last else links, between)
+        if not last:
+            for row in linked:
+                sweep(order, row)
 
 
 def sum_kernel(
     sky, inner,
-    fields, split, edge_split, fresh_second, fresh_third, last_links, acts, left,
+    split, edge_split, second, third, last_links, acts, inner_sums, left,
     flat, total,
-    full, second, third, part_in, part_out, in_send, in_recv, out_send, out_recv,
+    newest, part_in, part_out, in_send, in_recv, out_send, out_recv,
 ):
     rows, stacked, columns = split.shape
     orders = HALO + 1
@@ -344,45 +380,28 @@
     for peer in peers:
         pl.semaphore_signal(barrier, inc=1, device_id={"sky": peer}, device_id_type=MESH)
 
-    for depth in range(HALO + 1):
-        first = channels * TERMS.index((min(depth + 1, orders - 1), 0))
-        known = channels * TERMS.index((orders - 1, 0))
-        for side in range(2):
-            row = depth if side == 0 else rows - 1 - depth
-            if depth < HALO:
-                at = depth if side == 0 else 2 * HALO - 1 - depth
-                full[at, 0:first] = split[row, 0:first]
-                if first < known:
-                    full[at, first:known] = edge_split[at, first:known]
-                old = depth >= orders - 3
-                second[side, depth] = fields[orders - 3, HALO + row] if old else fresh_second[side, depth]
-            old = depth >= orders - 2
-            third[side, depth] = fields[orders - 2, HALO + row] if old else fresh_third[side, depth]
-
     for side in range(2):
-        def edge(depth):
-            return full.at[depth if side == 0 else 2 * HALO - 1 - depth]
-
         sweep_row(
             orders - 1, None, third.at[side, 0], third.at[side, 1], second.at[side, 0],
-            link=last_links.at[side], split=edge(0),
+            link=last_links.at[side], split=newest.at[side], start=0,
         )
-
-        @pl.loop(1, HALO)
-        def _(depth):
-            sweep_row(
-                orders - 1, third.at[side, depth - 1], third.at[side, depth], third.at[side, depth + 1],
-                second.at[side, depth], split=edge(depth),
-            )
 
     def edge_rows():
         return [(r, r) for r in range(HALO)] + [(rows - 2 * HALO + r, r) for r in range(HALO, 2 * HALO)]
 
-    sums = jnp.zeros((acts.shape[1], stacked), F32)
-    for r in range(HALO, rows - HALO):
-        sums += lax.dot_general(acts[r], split[r], CONTRACT_LAST, preferred_element_type=F32)
+    known = stacked - newest.shape[1]
+    outermost = {0: 0, rows - 1: 1}
+    sums = inner_sums[...]
     for r, at in edge_rows():
-        sums += lax.dot_general(acts[r], full[at], CONTRACT_LAST, preferred_element_type=F32)
+        if r not in outermost:
+            sums += lax.dot_general(acts[r], edge_split[at], CONTRACT_LAST, preferred_element_type=F32)
+    old_sums = jnp.zeros((acts.shape[1], known), F32)
+    new_sums = jnp.zeros((acts.shape[1], stacked - known), F32)
+    for r, at in edge_rows():
+        if r in outermost:
+            old_sums += lax.dot_general(acts[r], edge_split[at, 0:known], CONTRACT_LAST, preferred_element_type=F32)
+            new_sums += lax.dot_general(acts[r], newest[outermost[r]], CONTRACT_LAST, preferred_element_type=F32)
+    sums += jnp.concatenate([old_sums, new_sums], axis=1)
     part_in[slot] = sums[0:channels] + sums[channels : 2 * channels]
     pl.semaphore_wait(barrier, len(peers))
 
@@ -402,7 +421,12 @@
 
     copies = exchange(part_in, slot, inner, in_peer, in_send, in_recv)
     for r, at in edge_rows():
-        flat[:, r, :] = jnp.dot(left[...], full[at], preferred_element_type=F32)
+        if r in outermost:
+            flat[:, r, :] = jnp.dot(left[:, :known], edge_split[at, 0:known], preferred_element_type=F32) + jnp.dot(
+                left[:, known:], newest[outermost[r]], preferred_element_type=F32
+            )
+        else:
+            flat[:, r, :] = jnp.dot(left[...], edge_split[at], preferred_element_type=F32)
     part_out[group] = total_of(part_in, copies)
     copies = exchange(part_out, group, outer, out_peer, out_send, out_recv)
     for r in range(HALO, rows - HALO):
@@ -410,21 +434,14 @@
     total[...] = total_of(part_out, copies)
 
 
-def result_kernel(norm, flat, total, out, weight_grad, rounded, store):
-    channels = flat.shape[0]
-    copies = []
-    for start in range(0, channels, 4):
-        for channel in range(start, start + 4):
-            rounded[channel] = flat[channel].astype(BF16)
-        part = pl.ds(start, 4)
-        copies.append(pltpu.make_async_copy(rounded.at[part], out.at[part], store.at[start // 4]))
-        copies[-1].start()
+def result_kernel(norm, flat, total, out, weight_grad):
+    channels = out.shape[0]
+    for channel in range(channels):
+        out[channel] = flat[channel].astype(BF16)
     scaled = total[...] * norm
     for k in range(weight_grad.shape[0]):
         parts = [scaled[:, channels * i : channels * (i + 1)] for i, (order, _) in enumerate(TERMS) if order == k]
         weight_grad[k] = functools.reduce(jnp.add, parts)
-    for copy in copies:
-        copy.wait()
 
 
 def on_device(sky, saved_acts, scales, grad_out, weights, edge_up, edge_down):
@@ -443,19 +460,20 @@
     dma = pltpu.SemaphoreType.DMA
     shape = jax.ShapeDtypeStruct
     up, down = jnp.transpose(edge_up, (1, 0, 2)), jnp.transpose(edge_down, (1, 0, 2))
-    fields, split, acts, slots, codes, tables, left = pl.pallas_call(
+    fields, split, acts, sums, slots, codes, tables, left = pl.pallas_call(
         functools.partial(exchange_kernel, sky),
         out_shape=(
             shape((orders - 1, rows + 2 * HALO, channels, columns), F32),
             shape((rows, stacked, columns), BF16),
             shape((rows, 2 * channels, columns), BF16),
+            shape((2 * channels, stacked), F32),
             shape((4, columns // LANES, LANES), jnp.int32),
             shape((4, 3, columns // LANES, LANES), jnp.int32),
             shape((4, 3, 1, columns), jnp.int32),
             shape((channels, stacked), BF16),
         ),
         in_specs=[hbm] * 6,
-        out_specs=(vmem,) * 7,
+        out_specs=(vmem,) * 8,
         scratch_shapes=[
             pltpu.VMEM((channels, rows, columns), BF16),
             pltpu.VMEM((channels, rows, blocks), F32),
@@ -473,14 +491,14 @@
         name="exchange",
     )(*(pltpu.with_memory_space_constraint(x, pltpu.HBM) for x in (saved_acts, scales, grad_out, weights, up, down)))
     edge_split, second, third, last_links = pl.pallas_call(
-        functools.partial(edge_kernel, rows),
+        edge_kernel,
         out_shape=(
-            shape((edge, known, columns), BF16),
-            shape((2, HALO - 2, channels, columns), F32),
-            shape((2, HALO - 1, channels, columns), F32),
+            shape((edge, stacked, columns), BF16),
+            shape((2, HALO, channels, columns), F32),
+            shape((2, HALO + 1, channels, columns), F32),
             shape((2, channels, columns), F32),
         ),
-        in_specs=[vmem, smem, vmem, vmem],
+        in_specs=[vmem, vmem, smem, vmem, vmem],
         out_specs=(vmem,) * 4,
         scratch_shapes=[
             pltpu.VMEM((orders - 2, 2, HALO + 1, channels, columns), F32),
@@ -489,16 +507,14 @@
         ],
         compiler_params=pltpu.CompilerParams(vmem_limit_bytes=12 * 2**20),
         name="edges",
-    )(fields, slots, codes, tables)
+    )(fields, split, slots, codes, tables)
     flat, total = pl.pallas_call(
         functools.partial(sum_kernel, sky, inner),
         out_shape=(shape((channels, rows, columns), F32), shape((channels, stacked), F32)),
         in_specs=[vmem] * 8,
         out_specs=(vmem, vmem),
         scratch_shapes=[
-            pltpu.VMEM((edge, stacked, columns), BF16),
-            pltpu.VMEM((2, HALO, channels, columns), F32),
-            pltpu.VMEM((2, HALO + 1, channels, columns), F32),
+            pltpu.VMEM((2, stacked - known, columns), BF16),
             pltpu.VMEM((inner, channels, stacked), F32),
             pltpu.VMEM((outer, channels, stacked), F32),
             dma((inner,)), dma((inner,)), dma((outer,)), dma((outer,)),
@@ -507,13 +523,12 @@
             collective_id=1, has_side_effects=True, vmem_limit_bytes=12 * 2**20
         ),
         name="sky_sum",
-    )(fields, split, edge_split, second, third, last_links, acts, left)
+    )(split, edge_split, second, third, last_links, acts, sums, left)
     return pl.pallas_call(
         functools.partial(result_kernel, norm),
         out_shape=(shape((channels, rows, columns), BF16), shape((orders, channels, channels), F32)),
         in_specs=[vmem] * 2,
-        out_specs=(hbm, vmem),
-        scratch_shapes=[pltpu.VMEM((channels, rows, columns), BF16), dma((channels // 4,))],
+        out_specs=(vmem, vmem),
         compiler_params=pltpu.CompilerParams(vmem_limit_bytes=12 * 2**20),
         name="results",
     )(flat, total)

time: 41.8 us -> 39 us (0.933)
  Pallas kernels: 40.3 us -> 38 us
    pallas_call x1, Pallas kernels: 13.8 us -> 10.7 us  [on_device(): pl.pallas_call(functools.partial(sum_kernel, sky, inner), out_shape=(shap...]
    pallas_call x1, Pallas kernels: 17.4 us -> 18.3 us  [on_device(): pl.pallas_call(functools.partial(exchange_kernel, sky), out_shape=(shape(...]
    pallas_call x1, Pallas kernels: 1.69 us -> 1.13 us  [on_device(): pl.pallas_call(functools.partial(result_kernel, norm), out_shape=(shape((...]
    pallas_call x1, Pallas kernels: 7.4 us -> 7.86 us  [on_device(): pl.pallas_call(edge_kernel, out_shape=(shape((edge, stacked, columns), BF...]
where the time goes in v5:
time: 39 us; the launch traced here: 38.7 us
  Pallas kernels  38 us (97%)
  between operations  0.66 us (2%)
    pallas_call x1, Pallas kernels, on_device(): pl.pallas_call(functools.partial(exchange_kernel, sky), out_shape=(shape(...  18.3 us
    pallas_call x1, Pallas kernels, on_device(): pl.pallas_call(functools.partial(sum_kernel, sky, inner), out_shape=(shap...  10.7 us
    pallas_call x1, Pallas kernels, on_device(): pl.pallas_call(edge_kernel, out_shape=(shape((edge, stacked, columns), BF...  7.86 us
    pallas_call x1, Pallas kernels, on_device(): pl.pallas_call(functools.partial(result_kernel, norm), out_shape=(shape((...  1.13 us

profile of v5, /device:TPU:4, one launch (start us, length us, event | category | flops | bytes accessed | tf_op | source)
XLA Modules:
  0.0 38.7 jit_solution(2212571030789448702)
XLA Ops:
  0.6 18.3 %exchange.1 = (f32[4,24,16,2048]{3,2,1,0:T(8,128)S(1)}, bf16[16,128,2048]{2,1,0:T(8,128)(2,1)S(1)}, bf16[16,32,2048]{2,1,0:T(8,128)(2,1)S(1)}, f32[32,128]{1,0:T...) custom-call(bf16[16,16,2048]{2,1,0:T(8,128)(2,1)} %saved_hbm.1, ...), custom_call_target="tpu_custom_call" | custom-call | tf_op jit(solution)/shard_map/exchange/pallas_call | solution.py:463
  18.9 7.9 %edges.1 = (bf16[8,128,2048]{2,1,0:T(8,128)(2,1)S(1)}, f32[2,4,16,2048]{3,2,1,0:T(8,128)S(1)}, f32[2,5,16,2048]{3,2,1,0:T(8,128)S(1)}, f32[2,16,2048]{2,1,0:T(8,128)S(1)}) custom-call(f32[4,24,16,2048]{3,2,1,0:T(8,128)S(1)} %get-tuple-element.17.fields, bf16[16,128,2048]{2,1,0:T(8,128)(2,1)S(1)} %get-tuple-element.16.inner_split.split, ...), custom_call_target="tpu_custom_call" | custom-call | tf_op jit(solution)/shard_map/edges/pallas_call | solution.py:493
  26.8 10.7 %sky_sum.1 = (f32[16,16,2048]{2,1,0:T(8,128)S(1)}, f32[16,128]{1,0:T(8,128)S(1)}) custom-call(bf16[16,128,2048]{2,1,0:T(8,128)(2,1)S(1)} %get-tuple-element.16.inner_split.split, bf16[8,128,2048]{2,1,0:T(8,128)(2,1)S(1)} %get-tuple-element.21.edge_split, f32[2,4,16,2048]{3,2,1,0:T(8,128)S(1)} %get-tuple-element.22.second, ...), custom_call_target="tpu_custom_call" | custom-call | tf_op jit(solution)/shard_map/sky_sum/pallas_call | solution.py:511
  37.6 1.1 %results.1 = (bf16[16,16,2048]{2,1,0:T(8,128)(2,1)}, f32[5,16,16]{2,1,0:T(8,128)}) custom-call(f32[16,16,2048]{2,1,0:T(8,128)S(1)} %get-tuple-element.28.flat, f32[16,128]{1,0:T(8,128)S(1)} %get-tuple-element.29.total), custom_call_target="tpu_custom_call" | custom-call | tf_op jit(solution)/shard_map/results/pallas_call | solution.py:527

commit v6 on v5

--- a/solution.py
+++ b/solution.py
@@ -249,10 +249,10 @@
             total = None
             for entry in range(3):
                 first, second = slots[which, block, entry], slots[which, block, 3 + entry]
-                code = jnp.broadcast_to(codes[which, entry, block : block + 1, :], (2 * half, LANES))
+                code = jnp.broadcast_to(codes[which, entry, block : block + 1, :], (half, LANES))
+                lane = jnp.bitwise_and(code, LANES - 1)
                 values = jnp.concatenate([packed[which, first], packed[which, second]], axis=0)
-                arrived = moved(values, jnp.bitwise_and(code, LANES - 1))
-                code = code[:half]
+                arrived = moved(values, jnp.concatenate([lane, lane], axis=0))
                 picked = jnp.where(code < LANES, arrived[:half], jnp.where(code < 2 * LANES, arrived[half:], 0))
                 total = picked if total is None else total + picked
             put(which, out_lanes, total, steps[which])
@@ -355,11 +355,15 @@
                 sweep(order, row)
 
 
+def farthest_first(count):
+    return sorted(range(1, count), key=lambda step: -min(step, count - step))
+
+
 def sum_kernel(
     sky, inner,
     split, edge_split, second, third, last_links, acts, inner_sums, left,
-    flat, total,
-    newest, part_in, part_out, in_send, in_recv, out_send, out_recv,
+    rounded, total,
+    flat, newest, part_in, part_out, in_send, in_recv, out_send, out_recv,
 ):
     rows, stacked, columns = split.shape
     orders = HALO + 1
@@ -376,7 +380,7 @@
         return lax.rem(group + step, outer) * inner + slot
 
     barrier = pltpu.get_barrier_semaphore()
-    peers = [in_peer(step) for step in range(1, inner)] + [out_peer(step) for step in range(1, outer)]
+    peers = [out_peer(step) for step in farthest_first(outer)] + [in_peer(step) for step in farthest_first(inner)]
     for peer in peers:
         pl.semaphore_signal(barrier, inc=1, device_id={"sky": peer}, device_id_type=MESH)
 
@@ -408,7 +412,7 @@
     def exchange(buffer, own, count, peer_of, send, recv):
         copies = [
             remote(buffer.at[own], buffer.at[own], send.at[step], recv.at[step], peer_of(step))
-            for step in range(1, count)
+            for step in farthest_first(count)
         ]
         for copy in copies:
             copy.start()
@@ -431,13 +435,14 @@
     copies = exchange(part_out, group, outer, out_peer, out_send, out_recv)
     for r in range(HALO, rows - HALO):
         flat[:, r, :] = jnp.dot(left[...], split[r], preferred_element_type=F32)
+    for channel in range(channels):
+        rounded[channel] = flat[channel].astype(BF16)
     total[...] = total_of(part_out, copies)
 
 
-def result_kernel(norm, flat, total, out, weight_grad):
+def result_kernel(norm, rounded, total, out, weight_grad):
     channels = out.shape[0]
-    for channel in range(channels):
-        out[channel] = flat[channel].astype(BF16)
+    out[...] = rounded[...]
     scaled = total[...] * norm
     for k in range(weight_grad.shape[0]):
         parts = [scaled[:, channels * i : channels * (i + 1)] for i, (order, _) in enumerate(TERMS) if order == k]
@@ -508,12 +513,13 @@
         compiler_params=pltpu.CompilerParams(vmem_limit_bytes=12 * 2**20),
         name="edges",
     )(fields, split, slots, codes, tables)
-    flat, total = pl.pallas_call(
+    rounded, total = pl.pallas_call(
         functools.partial(sum_kernel, sky, inner),
-        out_shape=(shape((channels, rows, columns), F32), shape((channels, stacked), F32)),
+        out_shape=(shape((channels, rows, columns), BF16), shape((channels, stacked), F32)),
         in_specs=[vmem] * 8,
         out_specs=(vmem, vmem),
         scratch_shapes=[
+            pltpu.VMEM((channels, rows, columns), F32),
             pltpu.VMEM((2, stacked - known, columns), BF16),
             pltpu.VMEM((inner, channels, stacked), F32),
             pltpu.VMEM((outer, channels, stacked), F32),
@@ -531,7 +537,7 @@
         out_specs=(vmem, vmem),
         compiler_params=pltpu.CompilerParams(vmem_limit_bytes=12 * 2**20),
         name="results",
-    )(flat, total)
+    )(rounded, total)
 
 
 def solution(mesh):

time: 39 us -> 38.6 us (0.990)
  Pallas kernels: 38 us -> 37.4 us
    pallas_call x1, Pallas kernels: 10.7 us -> 10.3 us  [on_device(): pl.pallas_call(functools.partial(sum_kernel, sky, inner), out_shape=(shap...]
where the time goes in v6:
time: 38.6 us; the launch traced here: 38.1 us
  Pallas kernels  37.4 us (97%)
  between operations  0.66 us (2%)
    pallas_call x1, Pallas kernels, on_device(): pl.pallas_call(functools.partial(exchange_kernel, sky), out_shape=(shape(...  18.3 us
    pallas_call x1, Pallas kernels, on_device(): pl.pallas_call(functools.partial(sum_kernel, sky, inner), out_shape=(shap...  10.3 us
    pallas_call x1, Pallas kernels, on_device(): pl.pallas_call(edge_kernel, out_shape=(shape((edge, stacked, columns), BF...  7.8 us
    pallas_call x1, Pallas kernels, on_device(): pl.pallas_call(functools.partial(result_kernel, norm), out_shape=(shape((...  1.05 us

profile of v6, /device:TPU:4, one launch (start us, length us, event | category | flops | bytes accessed | tf_op | source)
XLA Modules:
  0.0 38.1 jit_solution(11563397040858901583)
XLA Ops:
  0.6 18.3 %exchange.1 = (f32[4,24,16,2048]{3,2,1,0:T(8,128)S(1)}, bf16[16,128,2048]{2,1,0:T(8,128)(2,1)S(1)}, bf16[16,32,2048]{2,1,0:T(8,128)(2,1)S(1)}, f32[32,128]{1,0:T...) custom-call(bf16[16,16,2048]{2,1,0:T(8,128)(2,1)} %saved_hbm.1, ...), custom_call_target="tpu_custom_call" | custom-call | tf_op jit(solution)/shard_map/exchange/pallas_call | solution.py:468
  18.9 7.8 %edges.1 = (bf16[8,128,2048]{2,1,0:T(8,128)(2,1)S(1)}, f32[2,4,16,2048]{3,2,1,0:T(8,128)S(1)}, f32[2,5,16,2048]{3,2,1,0:T(8,128)S(1)}, f32[2,16,2048]{2,1,0:T(8,128)S(1)}) custom-call(f32[4,24,16,2048]{3,2,1,0:T(8,128)S(1)} %get-tuple-element.17.fields, bf16[16,128,2048]{2,1,0:T(8,128)(2,1)S(1)} %get-tuple-element.16.inner_split.split, ...), custom_call_target="tpu_custom_call" | custom-call | tf_op jit(solution)/shard_map/edges/pallas_call | solution.py:498
  26.7 10.3 %sky_sum.1 = (bf16[16,16,2048]{2,1,0:T(8,128)(2,1)S(1)}, f32[16,128]{1,0:T(8,128)S(1)}) custom-call(bf16[16,128,2048]{2,1,0:T(8,128)(2,1)S(1)} %get-tuple-element.16.inner_split.split, bf16[8,128,2048]{2,1,0:T(8,128)(2,1)S(1)} %get-tuple-element.21.edge_split, f32[2,4,16,2048]{3,2,1,0:T(8,128)S(1)} %get-tuple-element.22.second, ...), custom_call_target="tpu_custom_call" | custom-call | tf_op jit(solution)/shard_map/sky_sum/pallas_call | solution.py:516
  37.0 1.1 %results.1 = (bf16[16,16,2048]{2,1,0:T(8,128)(2,1)}, f32[5,16,16]{2,1,0:T(8,128)}) custom-call(bf16[16,16,2048]{2,1,0:T(8,128)(2,1)S(1)} %get-tuple-element.28.rounded, f32[16,128]{1,0:T(8,128)S(1)} %get-tuple-element.29.total), custom_call_target="tpu_custom_call" | custom-call | tf_op jit(solution)/shard_map/results/pallas_call | solution.py:533

commit v7 on v6

--- a/solution.py
+++ b/solution.py
@@ -384,12 +384,6 @@
     for peer in peers:
         pl.semaphore_signal(barrier, inc=1, device_id={"sky": peer}, device_id_type=MESH)
 
-    for side in range(2):
-        sweep_row(
-            orders - 1, None, third.at[side, 0], third.at[side, 1], second.at[side, 0],
-            link=last_links.at[side], split=newest.at[side], start=0,
-        )
-
     def edge_rows():
         return [(r, r) for r in range(HALO)] + [(rows - 2 * HALO + r, r) for r in range(HALO, 2 * HALO)]
 
@@ -404,6 +398,13 @@
     for r, at in edge_rows():
         if r in outermost:
             old_sums += lax.dot_general(acts[r], edge_split[at, 0:known], CONTRACT_LAST, preferred_element_type=F32)
+    for side in range(2):
+        sweep_row(
+            orders - 1, None, third.at[side, 0], third.at[side, 1], second.at[side, 0],
+            link=last_links.at[side], split=newest.at[side], start=0,
+        )
+    for r, at in edge_rows():
+        if r in outermost:
             new_sums += lax.dot_general(acts[r], newest[outermost[r]], CONTRACT_LAST, preferred_element_type=F32)
     sums += jnp.concatenate([old_sums, new_sums], axis=1)
     part_in[slot] = sums[0:channels] + sums[channels : 2 * channels]

time: 38.6 us -> 38.6 us (level)
  no operation moved by 1% of the time
where the time goes in v7:
time: 38.6 us; the launch traced here: 38.1 us
  Pallas kernels  37.4 us (97%)
  between operations  0.66 us (2%)
    pallas_call x1, Pallas kernels, on_device(): pl.pallas_call(functools.partial(exchange_kernel, sky), out_shape=(shape(...  18.3 us
    pallas_call x1, Pallas kernels, on_device(): pl.pallas_call(functools.partial(sum_kernel, sky, inner), out_shape=(shap...  10.3 us
    pallas_call x1, Pallas kernels, on_device(): pl.pallas_call(edge_kernel, out_shape=(shape((edge, stacked, columns), BF...  7.81 us
    pallas_call x1, Pallas kernels, on_device(): pl.pallas_call(functools.partial(result_kernel, norm), out_shape=(shape((...  1.05 us

profile of v7, /device:TPU:4, one launch (start us, length us, event | category | flops | bytes accessed | tf_op | source)
XLA Modules:
  0.0 38.1 jit_solution(11343528007753006195)
XLA Ops:
  0.6 18.3 %exchange.1 = (f32[4,24,16,2048]{3,2,1,0:T(8,128)S(1)}, bf16[16,128,2048]{2,1,0:T(8,128)(2,1)S(1)}, bf16[16,32,2048]{2,1,0:T(8,128)(2,1)S(1)}, f32[32,128]{1,0:T...) custom-call(bf16[16,16,2048]{2,1,0:T(8,128)(2,1)} %saved_hbm.1, ...), custom_call_target="tpu_custom_call" | custom-call | tf_op jit(solution)/shard_map/exchange/pallas_call | solution.py:469
  18.9 7.8 %edges.1 = (bf16[8,128,2048]{2,1,0:T(8,128)(2,1)S(1)}, f32[2,4,16,2048]{3,2,1,0:T(8,128)S(1)}, f32[2,5,16,2048]{3,2,1,0:T(8,128)S(1)}, f32[2,16,2048]{2,1,0:T(8,128)S(1)}) custom-call(f32[4,24,16,2048]{3,2,1,0:T(8,128)S(1)} %get-tuple-element.17.fields, bf16[16,128,2048]{2,1,0:T(8,128)(2,1)S(1)} %get-tuple-element.16.inner_split.split, ...), custom_call_target="tpu_custom_call" | custom-call | tf_op jit(solution)/shard_map/edges/pallas_call | solution.py:499
  26.7 10.3 %sky_sum.1 = (bf16[16,16,2048]{2,1,0:T(8,128)(2,1)S(1)}, f32[16,128]{1,0:T(8,128)S(1)}) custom-call(bf16[16,128,2048]{2,1,0:T(8,128)(2,1)S(1)} %get-tuple-element.16.inner_split.split, bf16[8,128,2048]{2,1,0:T(8,128)(2,1)S(1)} %get-tuple-element.21.edge_split, f32[2,4,16,2048]{3,2,1,0:T(8,128)S(1)} %get-tuple-element.22.second, ...), custom_call_target="tpu_custom_call" | custom-call | tf_op jit(solution)/shard_map/sky_sum/pallas_call | solution.py:517
  37.0 1.1 %results.1 = (bf16[16,16,2048]{2,1,0:T(8,128)(2,1)}, f32[5,16,16]{2,1,0:T(8,128)}) custom-call(bf16[16,16,2048]{2,1,0:T(8,128)(2,1)S(1)} %get-tuple-element.28.rounded, f32[16,128]{1,0:T(8,128)S(1)} %get-tuple-element.29.total), custom_call_target="tpu_custom_call" | custom-call | tf_op jit(solution)/shard_map/results/pallas_call | solution.py:534
